TPU v7x, 512 devices: a whole 4x8x8 slice. The times are simulated.
512 devices in a mesh: section: 32 (over y_hi, z, core), dp: 16 (over x, y_lo).
Axes of the slice: x: 4, y: 8 (y_hi: 2, y_lo: 4; y = y_hi * 4 + y_lo), z: 8, core: 2. Of those that a mesh axis runs over, the one named last changes fastest.
Arguments:
- section_inputs: bfloat16 [32, 2048, 4096], P('section', 'dp'), may hold values from -6 to 6
- norm_gain: bfloat16 [32, 4096], P('section'), may hold values from 0.5 to 1.5
- down_proj: bfloat16 [32, 4096, 256], P('section', 'dp'), may hold values from -0.09375 to 0.09375
- up_proj: bfloat16 [32, 256, 4096], P('section', None, 'dp'), may hold values from -0.1875 to 0.1875
- readout_matrix: bfloat16 [4096, 128], P('dp'), may hold values from -0.09375 to 0.09375
- ground_truth_series: float32 [2048, 128], P('dp'), may hold values from -6 to 6
- valid_len: int32 [128], P('dp'), may hold values from 1 to 16
Outputs:
- input_grads: bfloat16 [32, 2048, 4096], P('section', 'dp')
- down_grads: bfloat16 [32, 4096, 256], P('section', 'dp')
- up_grads: bfloat16 [32, 256, 4096], P('section', None, 'dp')
All inputs are finite; a program needn't handle non-finite values.
Results may differ from a plain program's by a relative error of at most 0.035.
Values may be sent and summed in bfloat16 or wider, within the bound.
A program may use at most 64 MiB of HBM per device.

v0:
```python
import jax
import jax.numpy as jnp
from jax import lax
from jax.sharding import PartitionSpec as P

EPSILON = 1e-05


def from_behind(block, axis, distance):
    devices = range(lax.axis_size(axis))
    route = [(i - distance, i) for i in devices if i - distance in devices]
    return lax.ppermute(block, axis, route)


def normalize(inputs, gain_row):
    values = inputs.astype(jnp.float32)
    inverse = lax.rsqrt(jnp.mean(values * values, axis=-1, keepdims=True) + EPSILON)
    unit = values * inverse
    normed = (unit * gain_row.astype(jnp.float32)).astype(jnp.bfloat16)
    return (inverse, unit, normed)


def multiply_trailing_factor(left, right):
    return lax.dot_general(
        left, right, (((1,), (1,)), ((), ())), preferred_element_type=jnp.float32
    )


def contract_rows(left, right):
    return lax.dot_general(
        left, right, (((0,), (0,)), ((), ())), preferred_element_type=jnp.float32
    )


def block_backward(inverse, unit, latent, gain_row, down_full, up_full, arriving_gradient):
    sigmoid = jax.nn.sigmoid(latent)
    hidden_grad = multiply_trailing_factor(arriving_gradient, up_full)
    latent_grad = (hidden_grad * sigmoid * (1.0 + latent * (1.0 - sigmoid))).astype(jnp.bfloat16)
    scaled = multiply_trailing_factor(latent_grad, down_full) * gain_row.astype(jnp.float32)
    inputs_grad = arriving_gradient.astype(jnp.float32) + inverse * (
        scaled - unit * jnp.mean(scaled * unit, axis=-1, keepdims=True)
    )
    return (inputs_grad.astype(jnp.bfloat16), latent_grad)


def per_device(
    section_inputs, norm_gain, down_proj, up_proj, readout_matrix, ground_truth_series, valid_len
):
    down_full, up_full, entire_readout_matrix = (
        lax.all_gather(down_proj[0], "dp", axis=0, tiled=True),
        lax.all_gather(up_proj[0], "dp", axis=1, tiled=True),
        lax.all_gather(readout_matrix, "dp", axis=0, tiled=True),
    )
    inputs = section_inputs[0]
    gain_row = norm_gain[0]
    microbatch_count = valid_len.shape[0]
    token_count = inputs.shape[0]
    row_count = token_count // microbatch_count
    width = inputs.shape[1]
    latent_width = down_full.shape[1]
    inverse, unit, normed = normalize(inputs, gain_row)
    latent = jnp.dot(normed, down_full, preferred_element_type=jnp.float32)
    activated = jax.nn.silu(latent).astype(jnp.bfloat16)
    section_index = lax.axis_index("section")
    section_last = lax.axis_size("section") - 1
    observed_entry_indicator = (
        (jnp.arange(row_count)[None, :] < valid_len[:, None])
        .astype(jnp.float32)
        .reshape(token_count)
    )

    def loss_grad(unused):
        adapter_output = (
            inputs.astype(jnp.float32)
            + jnp.dot(activated, up_full, preferred_element_type=jnp.float32)
        ).astype(jnp.bfloat16)
        estimated_horizon = jnp.dot(
            adapter_output, entire_readout_matrix, preferred_element_type=jnp.float32
        )
        prediction_discrepancy = (
            observed_entry_indicator[:, None] * (estimated_horizon - ground_truth_series)
        ).astype(jnp.bfloat16)
        return multiply_trailing_factor(prediction_discrepancy, entire_readout_matrix).astype(
            jnp.bfloat16
        )

    def no_loss(unused):
        return jnp.zeros((token_count, width), jnp.bfloat16)

    top_grads = lax.cond(section_index == section_last, loss_grad, no_loss, 0).reshape(
        microbatch_count, row_count, width
    )
    inverse_micro = inverse.reshape(microbatch_count, row_count, 1)
    unit_micro = unit.reshape(microbatch_count, row_count, width)
    latent_micro = latent.reshape(microbatch_count, row_count, latent_width)

    def tick(tick_num, carry):
        outgoing, grads_in, latent_grads, cotangents = carry
        received = from_behind(outgoing, "section", -1)
        micro_num = tick_num - (section_last - section_index)
        is_valid = (micro_num >= 0) & (micro_num < microbatch_count)
        picked = jnp.clip(micro_num, 0, microbatch_count - 1)

        def process(state):
            arrived, grads_prev, latent_prev, cotangent_prev = state
            top_piece = lax.dynamic_index_in_dim(top_grads, picked, 0, keepdims=False)
            arriving_gradient = jnp.where(section_index == section_last, top_piece, arrived)
            inputs_grad, latent_grad = block_backward(
                lax.dynamic_index_in_dim(inverse_micro, picked, 0, keepdims=False),
                lax.dynamic_index_in_dim(unit_micro, picked, 0, keepdims=False),
                lax.dynamic_index_in_dim(latent_micro, picked, 0, keepdims=False),
                gain_row,
                down_full,
                up_full,
                arriving_gradient,
            )
            grads_next = lax.dynamic_update_index_in_dim(grads_prev, inputs_grad, picked, 0)
            latent_next = lax.dynamic_update_index_in_dim(latent_prev, latent_grad, picked, 0)
            cotangent_next = lax.dynamic_update_index_in_dim(
                cotangent_prev, arriving_gradient, picked, 0
            )
            return (inputs_grad, grads_next, latent_next, cotangent_next)

        def skipped(state):
            return state

        return lax.cond(is_valid, process, skipped, (received, grads_in, latent_grads, cotangents))

    initial = (
        jnp.zeros((row_count, width), jnp.bfloat16),
        jnp.zeros((microbatch_count, row_count, width), jnp.bfloat16),
        jnp.zeros((microbatch_count, row_count, latent_width), jnp.bfloat16),
        jnp.zeros((microbatch_count, row_count, width), jnp.bfloat16),
    )
    tick_total = lax.axis_size("section") + microbatch_count - 1
    final_state = lax.fori_loop(0, tick_total, tick, initial)
    grads_in = final_state[1].reshape(1, token_count, width)
    latent_grads = final_state[2].reshape(token_count, latent_width)
    cotangents = final_state[3].reshape(token_count, width)
    down_sum = lax.psum_scatter(
        contract_rows(normed, latent_grads), "dp", scatter_dimension=0, tiled=True
    )
    activated_all = lax.all_gather(activated, "dp", axis=0, tiled=True)
    cotangent_cols = lax.all_to_all(cotangents, "dp", split_axis=1, concat_axis=0, tiled=True)
    up_sum = contract_rows(activated_all, cotangent_cols)
    down_grads = down_sum.astype(jnp.bfloat16)[None]
    up_grads = up_sum.astype(jnp.bfloat16)[None]
    return (grads_in, down_grads, up_grads)


def solution(mesh):
    placed = (
        P("section", "dp", None),
        P("section", None),
        P("section", "dp", None),
        P("section", None, "dp"),
        P("dp", None),
        P("dp", None),
        P("dp"),
    )
    return jax.shard_map(
        per_device,
        mesh=mesh,
        in_specs=placed,
        out_specs=(P("section", "dp", None), P("section", "dp", None), P("section", None, "dp")),
        check_vma=False,
    )
```

profile of v0, /device:TPU:448, one launch (start us, length us, event | category | flops | bytes accessed | tf_op | source)
XLA Modules:
  0.0 932.3 jit_solution(12533757512585029941)
XLA Ops:
  11.8 87.0 %all-gather.11.cloned.1.call-done = bf16[1,4096,256]{2,1,0:T(8,128)(2,1)} async-done(((bf16[1,256,256]{2,1,0:T(8,128)(2,1)}), bf16[1,4096,256]{2,1,0:T(8,128)(2,1)}) %all-gather.11.cloned.1.call-update) | async-done | bytes 2097168 | tf_op jit(solution)/shard_map/all_gather | solution.py:50
  98.8 3.1 multiply_convert_fusion.1
  103.7 80.8 %all-gather.7.cloned.1.call-done = bf16[4096,128]{1,0:T(8,128)(2,1)} async-done(((bf16[256,128]{1,0:T(8,128)(2,1)}), bf16[4096,128]{1,0:T(8,128)(2,1)}) %all-gather.7.cloned.1.call-update) | async-done | bytes 1048592 | tf_op jit(solution)/shard_map/all_gather | solution.py:52
  184.5 87.1 %all-gather.13.cloned.1.call-done = bf16[1,256,4096]{2,1,0:T(8,128)(2,1)} async-done(((bf16[1,256,256]{2,1,0:T(8,128)(2,1)}), bf16[1,256,4096]{2,1,0:T(8,128)(2,1)}) %all-gather.13.cloned.1.call-update) | async-done | bytes 2097168 | tf_op jit(solution)/shard_map/all_gather | solution.py:51
  275.1 521.3 %while.20 = (s32[]{:T(128)}, bf16[16,4096]{1,0:T(8,128)(2,1)S(1)}, bf16[8,16,4096]{2,1,0:T(8,128)(2,1)}, bf16[8,16,256]{2,1,0:T(8,128)(2,1)S(1)}, bf16[8,16,4096...) while((s32[]{:T(128)}, bf16[16,4096]{1,0:T(8,128)(2,1)S(1)}, ...), condition=%wide.region_7.8_spmd, body=%wide.region_3.7_spmd.sunk | while | flops 67805192 | bytes 15549357 | solution.py:136
  277.1 2.5 collective-permute-done
  279.6 3.8 collective-permute-start
  283.4 2.5 collective-permute-done
  285.9 3.8 collective-permute-start
  289.7 7.3 collective-permute-done
  299.0 10.7 %collective-permute-done = bf16[16,4096]{1,0:T(8,128)(2,1)S(1)} collective-permute-done((bf16[16,4096]{1,0:T(8,128)(2,1)S(1)}, bf16[16,4096]{1,0:T(8,128)(2,1)S(1)}, u32[]{:S(2)}, u32[]{:S(2)}) %collective-permute-start) | collective-permute-done | bytes 131104 | tf_op jit(solution)/shard_map/while/body/eval_jaxpr/ppermute | solution.py:12
  311.6 10.6 %collective-permute-done = bf16[16,4096]{1,0:T(8,128)(2,1)S(1)} collective-permute-done((bf16[16,4096]{1,0:T(8,128)(2,1)S(1)}, bf16[16,4096]{1,0:T(8,128)(2,1)S(1)}, u32[]{:S(2)}, u32[]{:S(2)}) %collective-permute-start) | collective-permute-done | bytes 131104 | tf_op jit(solution)/shard_map/while/body/eval_jaxpr/ppermute | solution.py:12
  322.2 1.9 collective-permute-start
  324.2 10.9 %collective-permute-done = bf16[16,4096]{1,0:T(8,128)(2,1)S(1)} collective-permute-done((bf16[16,4096]{1,0:T(8,128)(2,1)S(1)}, bf16[16,4096]{1,0:T(8,128)(2,1)S(1)}, u32[]{:S(2)}, u32[]{:S(2)}) %collective-permute-start) | collective-permute-done | bytes 131104 | tf_op jit(solution)/shard_map/while/body/eval_jaxpr/ppermute | solution.py:12
  335.1 1.9 collective-permute-start
  337.0 11.3 %collective-permute-done = bf16[16,4096]{1,0:T(8,128)(2,1)S(1)} collective-permute-done((bf16[16,4096]{1,0:T(8,128)(2,1)S(1)}, bf16[16,4096]{1,0:T(8,128)(2,1)S(1)}, u32[]{:S(2)}, u32[]{:S(2)}) %collective-permute-start) | collective-permute-done | bytes 131104 | tf_op jit(solution)/shard_map/while/body/eval_jaxpr/ppermute | solution.py:12
  348.4 1.9 collective-permute-start
  350.3 10.7 %collective-permute-done = bf16[16,4096]{1,0:T(8,128)(2,1)S(1)} collective-permute-done((bf16[16,4096]{1,0:T(8,128)(2,1)S(1)}, bf16[16,4096]{1,0:T(8,128)(2,1)S(1)}, u32[]{:S(2)}, u32[]{:S(2)}) %collective-permute-start) | collective-permute-done | bytes 131104 | tf_op jit(solution)/shard_map/while/body/eval_jaxpr/ppermute | solution.py:12
  363.0 10.4 %collective-permute-done = bf16[16,4096]{1,0:T(8,128)(2,1)S(1)} collective-permute-done((bf16[16,4096]{1,0:T(8,128)(2,1)S(1)}, bf16[16,4096]{1,0:T(8,128)(2,1)S(1)}, u32[]{:S(2)}, u32[]{:S(2)}) %collective-permute-start) | collective-permute-done | bytes 131104 | tf_op jit(solution)/shard_map/while/body/eval_jaxpr/ppermute | solution.py:12
  375.4 10.4 %collective-permute-done = bf16[16,4096]{1,0:T(8,128)(2,1)S(1)} collective-permute-done((bf16[16,4096]{1,0:T(8,128)(2,1)S(1)}, bf16[16,4096]{1,0:T(8,128)(2,1)S(1)}, u32[]{:S(2)}, u32[]{:S(2)}) %collective-permute-start) | collective-permute-done | bytes 131104 | tf_op jit(solution)/shard_map/while/body/eval_jaxpr/ppermute | solution.py:12
  385.8 1.9 collective-permute-start
  387.7 10.4 %collective-permute-done = bf16[16,4096]{1,0:T(8,128)(2,1)S(1)} collective-permute-done((bf16[16,4096]{1,0:T(8,128)(2,1)S(1)}, bf16[16,4096]{1,0:T(8,128)(2,1)S(1)}, u32[]{:S(2)}, u32[]{:S(2)}) %collective-permute-start) | collective-permute-done | bytes 131104 | tf_op jit(solution)/shard_map/while/body/eval_jaxpr/ppermute | solution.py:12
  400.0 10.4 %collective-permute-done = bf16[16,4096]{1,0:T(8,128)(2,1)S(1)} collective-permute-done((bf16[16,4096]{1,0:T(8,128)(2,1)S(1)}, bf16[16,4096]{1,0:T(8,128)(2,1)S(1)}, u32[]{:S(2)}, u32[]{:S(2)}) %collective-permute-start) | collective-permute-done | bytes 131104 | tf_op jit(solution)/shard_map/while/body/eval_jaxpr/ppermute | solution.py:12
  412.4 10.4 %collective-permute-done = bf16[16,4096]{1,0:T(8,128)(2,1)S(1)} collective-permute-done((bf16[16,4096]{1,0:T(8,128)(2,1)S(1)}, bf16[16,4096]{1,0:T(8,128)(2,1)S(1)}, u32[]{:S(2)}, u32[]{:S(2)}) %collective-permute-start) | collective-permute-done | bytes 131104 | tf_op jit(solution)/shard_map/while/body/eval_jaxpr/ppermute | solution.py:12
  424.7 10.4 %collective-permute-done = bf16[16,4096]{1,0:T(8,128)(2,1)S(1)} collective-permute-done((bf16[16,4096]{1,0:T(8,128)(2,1)S(1)}, bf16[16,4096]{1,0:T(8,128)(2,1)S(1)}, u32[]{:S(2)}, u32[]{:S(2)}) %collective-permute-start) | collective-permute-done | bytes 131104 | tf_op jit(solution)/shard_map/while/body/eval_jaxpr/ppermute | solution.py:12
  437.0 10.4 %collective-permute-done = bf16[16,4096]{1,0:T(8,128)(2,1)S(1)} collective-permute-done((bf16[16,4096]{1,0:T(8,128)(2,1)S(1)}, bf16[16,4096]{1,0:T(8,128)(2,1)S(1)}, u32[]{:S(2)}, u32[]{:S(2)}) %collective-permute-start) | collective-permute-done | bytes 131104 | tf_op jit(solution)/shard_map/while/body/eval_jaxpr/ppermute | solution.py:12
  449.4 10.4 %collective-permute-done = bf16[16,4096]{1,0:T(8,128)(2,1)S(1)} collective-permute-done((bf16[16,4096]{1,0:T(8,128)(2,1)S(1)}, bf16[16,4096]{1,0:T(8,128)(2,1)S(1)}, u32[]{:S(2)}, u32[]{:S(2)}) %collective-permute-start) | collective-permute-done | bytes 131104 | tf_op jit(solution)/shard_map/while/body/eval_jaxpr/ppermute | solution.py:12
  461.7 10.4 %collective-permute-done = bf16[16,4096]{1,0:T(8,128)(2,1)S(1)} collective-permute-done((bf16[16,4096]{1,0:T(8,128)(2,1)S(1)}, bf16[16,4096]{1,0:T(8,128)(2,1)S(1)}, u32[]{:S(2)}, u32[]{:S(2)}) %collective-permute-start) | collective-permute-done | bytes 131104 | tf_op jit(solution)/shard_map/while/body/eval_jaxpr/ppermute | solution.py:12
  474.0 17.0 %collective-permute-done = bf16[16,4096]{1,0:T(8,128)(2,1)S(1)} collective-permute-done((bf16[16,4096]{1,0:T(8,128)(2,1)S(1)}, bf16[16,4096]{1,0:T(8,128)(2,1)S(1)}, u32[]{:S(2)}, u32[]{:S(2)}) %collective-permute-start) | collective-permute-done | bytes 131104 | tf_op jit(solution)/shard_map/while/body/eval_jaxpr/ppermute | solution.py:12
  491.0 6.6 conditional.4
  499.6 10.4 %collective-permute-done = bf16[16,4096]{1,0:T(8,128)(2,1)S(1)} collective-permute-done((bf16[16,4096]{1,0:T(8,128)(2,1)S(1)}, bf16[16,4096]{1,0:T(8,128)(2,1)S(1)}, u32[]{:S(2)}, u32[]{:S(2)}) %collective-permute-start) | collective-permute-done | bytes 131104 | tf_op jit(solution)/shard_map/while/body/eval_jaxpr/ppermute | solution.py:12
  510.0 6.6 conditional.4
  518.5 10.4 %collective-permute-done = bf16[16,4096]{1,0:T(8,128)(2,1)S(1)} collective-permute-done((bf16[16,4096]{1,0:T(8,128)(2,1)S(1)}, bf16[16,4096]{1,0:T(8,128)(2,1)S(1)}, u32[]{:S(2)}, u32[]{:S(2)}) %collective-permute-start) | collective-permute-done | bytes 131104 | tf_op jit(solution)/shard_map/while/body/eval_jaxpr/ppermute | solution.py:12
  528.9 6.6 conditional.4
  537.5 10.4 %collective-permute-done = bf16[16,4096]{1,0:T(8,128)(2,1)S(1)} collective-permute-done((bf16[16,4096]{1,0:T(8,128)(2,1)S(1)}, bf16[16,4096]{1,0:T(8,128)(2,1)S(1)}, u32[]{:S(2)}, u32[]{:S(2)}) %collective-permute-start) | collective-permute-done | bytes 131104 | tf_op jit(solution)/shard_map/while/body/eval_jaxpr/ppermute | solution.py:12
  547.8 6.6 conditional.4
  556.4 10.4 %collective-permute-done = bf16[16,4096]{1,0:T(8,128)(2,1)S(1)} collective-permute-done((bf16[16,4096]{1,0:T(8,128)(2,1)S(1)}, bf16[16,4096]{1,0:T(8,128)(2,1)S(1)}, u32[]{:S(2)}, u32[]{:S(2)}) %collective-permute-start) | collective-permute-done | bytes 131104 | tf_op jit(solution)/shard_map/while/body/eval_jaxpr/ppermute | solution.py:12
  566.8 6.6 conditional.4
  575.4 10.3 %collective-permute-done = bf16[16,4096]{1,0:T(8,128)(2,1)S(1)} collective-permute-done((bf16[16,4096]{1,0:T(8,128)(2,1)S(1)}, bf16[16,4096]{1,0:T(8,128)(2,1)S(1)}, u32[]{:S(2)}, u32[]{:S(2)}) %collective-permute-start) | collective-permute-done | bytes 131104 | tf_op jit(solution)/shard_map/while/body/eval_jaxpr/ppermute | solution.py:12
  585.8 6.6 conditional.4
  594.4 10.3 %collective-permute-done = bf16[16,4096]{1,0:T(8,128)(2,1)S(1)} collective-permute-done((bf16[16,4096]{1,0:T(8,128)(2,1)S(1)}, bf16[16,4096]{1,0:T(8,128)(2,1)S(1)}, u32[]{:S(2)}, u32[]{:S(2)}) %collective-permute-start) | collective-permute-done | bytes 131104 | tf_op jit(solution)/shard_map/while/body/eval_jaxpr/ppermute | solution.py:12
  604.7 6.6 conditional.4
  613.3 10.4 %collective-permute-done = bf16[16,4096]{1,0:T(8,128)(2,1)S(1)} collective-permute-done((bf16[16,4096]{1,0:T(8,128)(2,1)S(1)}, bf16[16,4096]{1,0:T(8,128)(2,1)S(1)}, u32[]{:S(2)}, u32[]{:S(2)}) %collective-permute-start) | collective-permute-done | bytes 131104 | tf_op jit(solution)/shard_map/while/body/eval_jaxpr/ppermute | solution.py:12
  623.7 6.6 conditional.4
  632.2 3.8 collective-permute-done
  636.0 9.1 collective-permute-start
  645.2 3.2 collective-permute-done
  648.4 3.1 collective-permute-start
  651.5 9.2 collective-permute-done
  662.6 10.4 %collective-permute-done = bf16[16,4096]{1,0:T(8,128)(2,1)S(1)} collective-permute-done((bf16[16,4096]{1,0:T(8,128)(2,1)S(1)}, bf16[16,4096]{1,0:T(8,128)(2,1)S(1)}, u32[]{:S(2)}, u32[]{:S(2)}) %collective-permute-start) | collective-permute-done | bytes 131104 | tf_op jit(solution)/shard_map/while/body/eval_jaxpr/ppermute | solution.py:12
  675.0 10.4 %collective-permute-done = bf16[16,4096]{1,0:T(8,128)(2,1)S(1)} collective-permute-done((bf16[16,4096]{1,0:T(8,128)(2,1)S(1)}, bf16[16,4096]{1,0:T(8,128)(2,1)S(1)}, u32[]{:S(2)}, u32[]{:S(2)}) %collective-permute-start) | collective-permute-done | bytes 131104 | tf_op jit(solution)/shard_map/while/body/eval_jaxpr/ppermute | solution.py:12
  687.3 10.4 %collective-permute-done = bf16[16,4096]{1,0:T(8,128)(2,1)S(1)} collective-permute-done((bf16[16,4096]{1,0:T(8,128)(2,1)S(1)}, bf16[16,4096]{1,0:T(8,128)(2,1)S(1)}, u32[]{:S(2)}, u32[]{:S(2)}) %collective-permute-start) | collective-permute-done | bytes 131104 | tf_op jit(solution)/shard_map/while/body/eval_jaxpr/ppermute | solution.py:12
  699.6 10.4 %collective-permute-done = bf16[16,4096]{1,0:T(8,128)(2,1)S(1)} collective-permute-done((bf16[16,4096]{1,0:T(8,128)(2,1)S(1)}, bf16[16,4096]{1,0:T(8,128)(2,1)S(1)}, u32[]{:S(2)}, u32[]{:S(2)}) %collective-permute-start) | collective-permute-done | bytes 131104 | tf_op jit(solution)/shard_map/while/body/eval_jaxpr/ppermute | solution.py:12
  712.0 10.4 %collective-permute-done = bf16[16,4096]{1,0:T(8,128)(2,1)S(1)} collective-permute-done((bf16[16,4096]{1,0:T(8,128)(2,1)S(1)}, bf16[16,4096]{1,0:T(8,128)(2,1)S(1)}, u32[]{:S(2)}, u32[]{:S(2)}) %collective-permute-start) | collective-permute-done | bytes 131104 | tf_op jit(solution)/shard_map/while/body/eval_jaxpr/ppermute | solution.py:12
  724.3 10.4 %collective-permute-done = bf16[16,4096]{1,0:T(8,128)(2,1)S(1)} collective-permute-done((bf16[16,4096]{1,0:T(8,128)(2,1)S(1)}, bf16[16,4096]{1,0:T(8,128)(2,1)S(1)}, u32[]{:S(2)}, u32[]{:S(2)}) %collective-permute-start) | collective-permute-done | bytes 131104 | tf_op jit(solution)/shard_map/while/body/eval_jaxpr/ppermute | solution.py:12
  736.6 10.4 %collective-permute-done = bf16[16,4096]{1,0:T(8,128)(2,1)S(1)} collective-permute-done((bf16[16,4096]{1,0:T(8,128)(2,1)S(1)}, bf16[16,4096]{1,0:T(8,128)(2,1)S(1)}, u32[]{:S(2)}, u32[]{:S(2)}) %collective-permute-start) | collective-permute-done | bytes 131104 | tf_op jit(solution)/shard_map/while/body/eval_jaxpr/ppermute | solution.py:12
  749.0 10.4 %collective-permute-done = bf16[16,4096]{1,0:T(8,128)(2,1)S(1)} collective-permute-done((bf16[16,4096]{1,0:T(8,128)(2,1)S(1)}, bf16[16,4096]{1,0:T(8,128)(2,1)S(1)}, u32[]{:S(2)}, u32[]{:S(2)}) %collective-permute-start) | collective-permute-done | bytes 131104 | tf_op jit(solution)/shard_map/while/body/eval_jaxpr/ppermute | solution.py:12
  761.3 10.4 %collective-permute-done = bf16[16,4096]{1,0:T(8,128)(2,1)S(1)} collective-permute-done((bf16[16,4096]{1,0:T(8,128)(2,1)S(1)}, bf16[16,4096]{1,0:T(8,128)(2,1)S(1)}, u32[]{:S(2)}, u32[]{:S(2)}) %collective-permute-start) | collective-permute-done | bytes 131104 | tf_op jit(solution)/shard_map/while/body/eval_jaxpr/ppermute | solution.py:12
  773.6 10.4 %collective-permute-done = bf16[16,4096]{1,0:T(8,128)(2,1)S(1)} collective-permute-done((bf16[16,4096]{1,0:T(8,128)(2,1)S(1)}, bf16[16,4096]{1,0:T(8,128)(2,1)S(1)}, u32[]{:S(2)}, u32[]{:S(2)}) %collective-permute-start) | collective-permute-done | bytes 131104 | tf_op jit(solution)/shard_map/while/body/eval_jaxpr/ppermute | solution.py:12
  786.0 10.4 %collective-permute-done = bf16[16,4096]{1,0:T(8,128)(2,1)S(1)} collective-permute-done((bf16[16,4096]{1,0:T(8,128)(2,1)S(1)}, bf16[16,4096]{1,0:T(8,128)(2,1)S(1)}, u32[]{:S(2)}, u32[]{:S(2)}) %collective-permute-start) | collective-permute-done | bytes 131104 | tf_op jit(solution)/shard_map/while/body/eval_jaxpr/ppermute | solution.py:12
  796.4 2.8 fusion.22
  801.0 43.8 %all_to_all.19 = bf16[128,16,256]{2,0,1:T(8,128)(2,1)S(1)} all-to-all(bf16[128,16,256]{2,0,1:T(8,128)(2,1)S(1)} %copy.16), channel_id=1, replica_groups=mesh['section'=32,'dp'=16] {'dp'}, dimensions={1} | all-to-all | bytes 2097152 | tf_op jit(solution)/shard_map/all_to_all | solution.py:144
  844.7 2.4 fusion.20
  847.1 77.1 %reduce-scatter.2.cloned.1.call-done = f32[256,256]{1,0:T(8,128)} async-done(((f32[4096,256]{1,0:T(8,128)}), f32[256,256]{1,0:T(8,128)}) %reduce-scatter.2.cloned.1.call-update) | async-done | bytes 262160 | tf_op jit(solution)/shard_map/reduce_scatter | solution.py:140
  (213 shorter events, 126.9 us)
Async XLA Ops:
  7.2 91.6 %all-gather.11.cloned.1.call-start = ((), (), s32[]{:S(2)}) async-start(), calls=%async_computation.5 | async-start | bytes 2228224 | tf_op jit(solution)/shard_map/all_gather | solution.py:50
  7.9 176.6 %all-gather.7.cloned.1.call-start = ((), (), s32[]{:S(2)}) async-start(), calls=%async_computation.2 | async-start | bytes 1114112 | tf_op jit(solution)/shard_map/all_gather | solution.py:52
  8.6 263.0 %all-gather.13.cloned.1.call-start = ((), (), s32[]{:S(2)}) async-start(), calls=%async_computation.6 | async-start | bytes 2228224 | tf_op jit(solution)/shard_map/all_gather | solution.py:51
  9.4 835.3 %all-gather.9.cloned.1.call-start = ((), (), s32[]{:S(2)}) async-start(), calls=%async_computation.4 | async-start | bytes 1114112 | tf_op jit(solution)/shard_map/all_gather | solution.py:143
  11.7 90.4 %copy-start.7 = (s32[8]{0:T(128)S(1)}, s32[8]{0:T(128)}, u32[]{:S(2)}) copy-start(s32[8]{0:T(128)} %param.19) | copy-start | bytes 100
  11.7 90.4 %copy-start.2 = (bf16[1,128,4096]{2,1,0:T(8,128)(2,1)S(1)}, bf16[1,128,4096]{2,1,0:T(8,128)(2,1)}, u32[]{:S(2)}) copy-start(bf16[1,128,4096]{2,1,0:T(8,128)(2,1)} %param.13) | copy-start | bytes 3145732
  101.9 169.8 %copy-start.5 = (bf16[128,256]{1,0:T(8,128)(2,1)S(1)}, bf16[128,256]{1,0:T(8,128)(2,1)}, u32[]{:S(2)}) copy-start(bf16[128,256]{1,0:T(8,128)(2,1)} %get-tuple-element.490) | copy-start | bytes 196612
  101.9 169.8 %copy-start.6 = (f32[128,128]{1,0:T(8,128)S(1)}, f32[128,128]{1,0:T(8,128)}, u32[]{:S(2)}) copy-start(f32[128,128]{1,0:T(8,128)} %param.18) | copy-start | bytes 196612
  101.9 822.3 %reduce-scatter.2.cloned.1.call-start = ((), (), s32[]{:S(2)}) async-start(), calls=%async_computation.3 | async-start | bytes 4456448 | tf_op jit(solution)/shard_map/reduce_scatter | solution.py:140
  272.8 2.3 copy-start
  275.1 4.4 collective-permute-start
  279.6 6.3 collective-permute-start
  285.9 11.1 %collective-permute-start = (bf16[16,4096]{1,0:T(8,128)(2,1)S(1)}, bf16[16,4096]{1,0:T(8,128)(2,1)S(1)}, u32[]{:S(2)}, u32[]{:S(2)}) collective-permute-start(bf16[16,4096]{1,0:T(8,128)(2,1)S(1)} %get-tuple-element.611), channel_id=1, source_target_pairs={{16,0},{32,16},{48,32},{64,48},{80,64},{96,80},{112,96},{128,112},... | collective-permute-start | bytes 393224 | tf_op jit(solution)/shard_map/while/body/eval_jaxpr/ppermute | solution.py:12
  297.0 12.7 %collective-permute-start = (bf16[16,4096]{1,0:T(8,128)(2,1)S(1)}, bf16[16,4096]{1,0:T(8,128)(2,1)S(1)}, u32[]{:S(2)}, u32[]{:S(2)}) collective-permute-start(bf16[16,4096]{1,0:T(8,128)(2,1)S(1)} %get-tuple-element.611), channel_id=1, source_target_pairs={{16,0},{32,16},{48,32},{64,48},{80,64},{96,80},{112,96},{128,112},... | collective-permute-start | bytes 393224 | tf_op jit(solution)/shard_map/while/body/eval_jaxpr/ppermute | solution.py:12
  309.7 12.5 %collective-permute-start = (bf16[16,4096]{1,0:T(8,128)(2,1)S(1)}, bf16[16,4096]{1,0:T(8,128)(2,1)S(1)}, u32[]{:S(2)}, u32[]{:S(2)}) collective-permute-start(bf16[16,4096]{1,0:T(8,128)(2,1)S(1)} %get-tuple-element.611), channel_id=1, source_target_pairs={{16,0},{32,16},{48,32},{64,48},{80,64},{96,80},{112,96},{128,112},... | collective-permute-start | bytes 393224 | tf_op jit(solution)/shard_map/while/body/eval_jaxpr/ppermute | solution.py:12
  322.2 12.8 %collective-permute-start = (bf16[16,4096]{1,0:T(8,128)(2,1)S(1)}, bf16[16,4096]{1,0:T(8,128)(2,1)S(1)}, u32[]{:S(2)}, u32[]{:S(2)}) collective-permute-start(bf16[16,4096]{1,0:T(8,128)(2,1)S(1)} %get-tuple-element.611), channel_id=1, source_target_pairs={{16,0},{32,16},{48,32},{64,48},{80,64},{96,80},{112,96},{128,112},... | collective-permute-start | bytes 393224 | tf_op jit(solution)/shard_map/while/body/eval_jaxpr/ppermute | solution.py:12
  335.1 13.3 %collective-permute-start = (bf16[16,4096]{1,0:T(8,128)(2,1)S(1)}, bf16[16,4096]{1,0:T(8,128)(2,1)S(1)}, u32[]{:S(2)}, u32[]{:S(2)}) collective-permute-start(bf16[16,4096]{1,0:T(8,128)(2,1)S(1)} %get-tuple-element.611), channel_id=1, source_target_pairs={{16,0},{32,16},{48,32},{64,48},{80,64},{96,80},{112,96},{128,112},... | collective-permute-start | bytes 393224 | tf_op jit(solution)/shard_map/while/body/eval_jaxpr/ppermute | solution.py:12
  348.4 12.7 %collective-permute-start = (bf16[16,4096]{1,0:T(8,128)(2,1)S(1)}, bf16[16,4096]{1,0:T(8,128)(2,1)S(1)}, u32[]{:S(2)}, u32[]{:S(2)}) collective-permute-start(bf16[16,4096]{1,0:T(8,128)(2,1)S(1)} %get-tuple-element.611), channel_id=1, source_target_pairs={{16,0},{32,16},{48,32},{64,48},{80,64},{96,80},{112,96},{128,112},... | collective-permute-start | bytes 393224 | tf_op jit(solution)/shard_map/while/body/eval_jaxpr/ppermute | solution.py:12
  361.1 12.3 %collective-permute-start = (bf16[16,4096]{1,0:T(8,128)(2,1)S(1)}, bf16[16,4096]{1,0:T(8,128)(2,1)S(1)}, u32[]{:S(2)}, u32[]{:S(2)}) collective-permute-start(bf16[16,4096]{1,0:T(8,128)(2,1)S(1)} %get-tuple-element.611), channel_id=1, source_target_pairs={{16,0},{32,16},{48,32},{64,48},{80,64},{96,80},{112,96},{128,112},... | collective-permute-start | bytes 393224 | tf_op jit(solution)/shard_map/while/body/eval_jaxpr/ppermute | solution.py:12
  373.4 12.3 %collective-permute-start = (bf16[16,4096]{1,0:T(8,128)(2,1)S(1)}, bf16[16,4096]{1,0:T(8,128)(2,1)S(1)}, u32[]{:S(2)}, u32[]{:S(2)}) collective-permute-start(bf16[16,4096]{1,0:T(8,128)(2,1)S(1)} %get-tuple-element.611), channel_id=1, source_target_pairs={{16,0},{32,16},{48,32},{64,48},{80,64},{96,80},{112,96},{128,112},... | collective-permute-start | bytes 393224 | tf_op jit(solution)/shard_map/while/body/eval_jaxpr/ppermute | solution.py:12
  385.8 12.3 %collective-permute-start = (bf16[16,4096]{1,0:T(8,128)(2,1)S(1)}, bf16[16,4096]{1,0:T(8,128)(2,1)S(1)}, u32[]{:S(2)}, u32[]{:S(2)}) collective-permute-start(bf16[16,4096]{1,0:T(8,128)(2,1)S(1)} %get-tuple-element.611), channel_id=1, source_target_pairs={{16,0},{32,16},{48,32},{64,48},{80,64},{96,80},{112,96},{128,112},... | collective-permute-start | bytes 393224 | tf_op jit(solution)/shard_map/while/body/eval_jaxpr/ppermute | solution.py:12
  398.1 12.3 %collective-permute-start = (bf16[16,4096]{1,0:T(8,128)(2,1)S(1)}, bf16[16,4096]{1,0:T(8,128)(2,1)S(1)}, u32[]{:S(2)}, u32[]{:S(2)}) collective-permute-start(bf16[16,4096]{1,0:T(8,128)(2,1)S(1)} %get-tuple-element.611), channel_id=1, source_target_pairs={{16,0},{32,16},{48,32},{64,48},{80,64},{96,80},{112,96},{128,112},... | collective-permute-start | bytes 393224 | tf_op jit(solution)/shard_map/while/body/eval_jaxpr/ppermute | solution.py:12
  410.4 12.3 %collective-permute-start = (bf16[16,4096]{1,0:T(8,128)(2,1)S(1)}, bf16[16,4096]{1,0:T(8,128)(2,1)S(1)}, u32[]{:S(2)}, u32[]{:S(2)}) collective-permute-start(bf16[16,4096]{1,0:T(8,128)(2,1)S(1)} %get-tuple-element.611), channel_id=1, source_target_pairs={{16,0},{32,16},{48,32},{64,48},{80,64},{96,80},{112,96},{128,112},... | collective-permute-start | bytes 393224 | tf_op jit(solution)/shard_map/while/body/eval_jaxpr/ppermute | solution.py:12
  422.8 12.3 %collective-permute-start = (bf16[16,4096]{1,0:T(8,128)(2,1)S(1)}, bf16[16,4096]{1,0:T(8,128)(2,1)S(1)}, u32[]{:S(2)}, u32[]{:S(2)}) collective-permute-start(bf16[16,4096]{1,0:T(8,128)(2,1)S(1)} %get-tuple-element.611), channel_id=1, source_target_pairs={{16,0},{32,16},{48,32},{64,48},{80,64},{96,80},{112,96},{128,112},... | collective-permute-start | bytes 393224 | tf_op jit(solution)/shard_map/while/body/eval_jaxpr/ppermute | solution.py:12
  435.1 12.3 %collective-permute-start = (bf16[16,4096]{1,0:T(8,128)(2,1)S(1)}, bf16[16,4096]{1,0:T(8,128)(2,1)S(1)}, u32[]{:S(2)}, u32[]{:S(2)}) collective-permute-start(bf16[16,4096]{1,0:T(8,128)(2,1)S(1)} %get-tuple-element.611), channel_id=1, source_target_pairs={{16,0},{32,16},{48,32},{64,48},{80,64},{96,80},{112,96},{128,112},... | collective-permute-start | bytes 393224 | tf_op jit(solution)/shard_map/while/body/eval_jaxpr/ppermute | solution.py:12
  447.4 12.3 %collective-permute-start = (bf16[16,4096]{1,0:T(8,128)(2,1)S(1)}, bf16[16,4096]{1,0:T(8,128)(2,1)S(1)}, u32[]{:S(2)}, u32[]{:S(2)}) collective-permute-start(bf16[16,4096]{1,0:T(8,128)(2,1)S(1)} %get-tuple-element.611), channel_id=1, source_target_pairs={{16,0},{32,16},{48,32},{64,48},{80,64},{96,80},{112,96},{128,112},... | collective-permute-start | bytes 393224 | tf_op jit(solution)/shard_map/while/body/eval_jaxpr/ppermute | solution.py:12
  459.8 12.3 %collective-permute-start = (bf16[16,4096]{1,0:T(8,128)(2,1)S(1)}, bf16[16,4096]{1,0:T(8,128)(2,1)S(1)}, u32[]{:S(2)}, u32[]{:S(2)}) collective-permute-start(bf16[16,4096]{1,0:T(8,128)(2,1)S(1)} %get-tuple-element.611), channel_id=1, source_target_pairs={{16,0},{32,16},{48,32},{64,48},{80,64},{96,80},{112,96},{128,112},... | collective-permute-start | bytes 393224 | tf_op jit(solution)/shard_map/while/body/eval_jaxpr/ppermute | solution.py:12
  472.1 18.9 %collective-permute-start = (bf16[16,4096]{1,0:T(8,128)(2,1)S(1)}, bf16[16,4096]{1,0:T(8,128)(2,1)S(1)}, u32[]{:S(2)}, u32[]{:S(2)}) collective-permute-start(bf16[16,4096]{1,0:T(8,128)(2,1)S(1)} %get-tuple-element.611), channel_id=1, source_target_pairs={{16,0},{32,16},{48,32},{64,48},{80,64},{96,80},{112,96},{128,112},... | collective-permute-start | bytes 393224 | tf_op jit(solution)/shard_map/while/body/eval_jaxpr/ppermute | solution.py:12
  491.0 3.1 copy-start.1
  497.7 12.3 %collective-permute-start = (bf16[16,4096]{1,0:T(8,128)(2,1)S(1)}, bf16[16,4096]{1,0:T(8,128)(2,1)S(1)}, u32[]{:S(2)}, u32[]{:S(2)}) collective-permute-start(bf16[16,4096]{1,0:T(8,128)(2,1)S(1)} %get-tuple-element.611), channel_id=1, source_target_pairs={{16,0},{32,16},{48,32},{64,48},{80,64},{96,80},{112,96},{128,112},... | collective-permute-start | bytes 393224 | tf_op jit(solution)/shard_map/while/body/eval_jaxpr/ppermute | solution.py:12
  510.0 3.1 copy-start.1
  516.6 12.3 %collective-permute-start = (bf16[16,4096]{1,0:T(8,128)(2,1)S(1)}, bf16[16,4096]{1,0:T(8,128)(2,1)S(1)}, u32[]{:S(2)}, u32[]{:S(2)}) collective-permute-start(bf16[16,4096]{1,0:T(8,128)(2,1)S(1)} %get-tuple-element.611), channel_id=1, source_target_pairs={{16,0},{32,16},{48,32},{64,48},{80,64},{96,80},{112,96},{128,112},... | collective-permute-start | bytes 393224 | tf_op jit(solution)/shard_map/while/body/eval_jaxpr/ppermute | solution.py:12
  528.9 3.1 copy-start.1
  535.5 12.3 %collective-permute-start = (bf16[16,4096]{1,0:T(8,128)(2,1)S(1)}, bf16[16,4096]{1,0:T(8,128)(2,1)S(1)}, u32[]{:S(2)}, u32[]{:S(2)}) collective-permute-start(bf16[16,4096]{1,0:T(8,128)(2,1)S(1)} %get-tuple-element.611), channel_id=1, source_target_pairs={{16,0},{32,16},{48,32},{64,48},{80,64},{96,80},{112,96},{128,112},... | collective-permute-start | bytes 393224 | tf_op jit(solution)/shard_map/while/body/eval_jaxpr/ppermute | solution.py:12
  547.8 3.1 copy-start.1
  554.5 12.3 %collective-permute-start = (bf16[16,4096]{1,0:T(8,128)(2,1)S(1)}, bf16[16,4096]{1,0:T(8,128)(2,1)S(1)}, u32[]{:S(2)}, u32[]{:S(2)}) collective-permute-start(bf16[16,4096]{1,0:T(8,128)(2,1)S(1)} %get-tuple-element.611), channel_id=1, source_target_pairs={{16,0},{32,16},{48,32},{64,48},{80,64},{96,80},{112,96},{128,112},... | collective-permute-start | bytes 393224 | tf_op jit(solution)/shard_map/while/body/eval_jaxpr/ppermute | solution.py:12
  566.8 3.1 copy-start.1
  573.5 12.3 %collective-permute-start = (bf16[16,4096]{1,0:T(8,128)(2,1)S(1)}, bf16[16,4096]{1,0:T(8,128)(2,1)S(1)}, u32[]{:S(2)}, u32[]{:S(2)}) collective-permute-start(bf16[16,4096]{1,0:T(8,128)(2,1)S(1)} %get-tuple-element.611), channel_id=1, source_target_pairs={{16,0},{32,16},{48,32},{64,48},{80,64},{96,80},{112,96},{128,112},... | collective-permute-start | bytes 393224 | tf_op jit(solution)/shard_map/while/body/eval_jaxpr/ppermute | solution.py:12
  585.8 3.1 copy-start.1
  592.4 12.3 %collective-permute-start = (bf16[16,4096]{1,0:T(8,128)(2,1)S(1)}, bf16[16,4096]{1,0:T(8,128)(2,1)S(1)}, u32[]{:S(2)}, u32[]{:S(2)}) collective-permute-start(bf16[16,4096]{1,0:T(8,128)(2,1)S(1)} %get-tuple-element.611), channel_id=1, source_target_pairs={{16,0},{32,16},{48,32},{64,48},{80,64},{96,80},{112,96},{128,112},... | collective-permute-start | bytes 393224 | tf_op jit(solution)/shard_map/while/body/eval_jaxpr/ppermute | solution.py:12
  604.7 3.1 copy-start.1
  611.3 12.3 %collective-permute-start = (bf16[16,4096]{1,0:T(8,128)(2,1)S(1)}, bf16[16,4096]{1,0:T(8,128)(2,1)S(1)}, u32[]{:S(2)}, u32[]{:S(2)}) collective-permute-start(bf16[16,4096]{1,0:T(8,128)(2,1)S(1)} %get-tuple-element.611), channel_id=1, source_target_pairs={{16,0},{32,16},{48,32},{64,48},{80,64},{96,80},{112,96},{128,112},... | collective-permute-start | bytes 393224 | tf_op jit(solution)/shard_map/while/body/eval_jaxpr/ppermute | solution.py:12
  623.7 3.1 copy-start.1
  630.3 5.7 collective-permute-start
  636.0 12.3 %collective-permute-start = (bf16[16,4096]{1,0:T(8,128)(2,1)S(1)}, bf16[16,4096]{1,0:T(8,128)(2,1)S(1)}, u32[]{:S(2)}, u32[]{:S(2)}) collective-permute-start(bf16[16,4096]{1,0:T(8,128)(2,1)S(1)} %get-tuple-element.611), channel_id=1, source_target_pairs={{16,0},{32,16},{48,32},{64,48},{80,64},{96,80},{112,96},{128,112},... | collective-permute-start | bytes 393224 | tf_op jit(solution)/shard_map/while/body/eval_jaxpr/ppermute | solution.py:12
  648.4 12.3 %collective-permute-start = (bf16[16,4096]{1,0:T(8,128)(2,1)S(1)}, bf16[16,4096]{1,0:T(8,128)(2,1)S(1)}, u32[]{:S(2)}, u32[]{:S(2)}) collective-permute-start(bf16[16,4096]{1,0:T(8,128)(2,1)S(1)} %get-tuple-element.611), channel_id=1, source_target_pairs={{16,0},{32,16},{48,32},{64,48},{80,64},{96,80},{112,96},{128,112},... | collective-permute-start | bytes 393224 | tf_op jit(solution)/shard_map/while/body/eval_jaxpr/ppermute | solution.py:12
  660.7 12.3 %collective-permute-start = (bf16[16,4096]{1,0:T(8,128)(2,1)S(1)}, bf16[16,4096]{1,0:T(8,128)(2,1)S(1)}, u32[]{:S(2)}, u32[]{:S(2)}) collective-permute-start(bf16[16,4096]{1,0:T(8,128)(2,1)S(1)} %get-tuple-element.611), channel_id=1, source_target_pairs={{16,0},{32,16},{48,32},{64,48},{80,64},{96,80},{112,96},{128,112},... | collective-permute-start | bytes 393224 | tf_op jit(solution)/shard_map/while/body/eval_jaxpr/ppermute | solution.py:12
  673.0 12.3 %collective-permute-start = (bf16[16,4096]{1,0:T(8,128)(2,1)S(1)}, bf16[16,4096]{1,0:T(8,128)(2,1)S(1)}, u32[]{:S(2)}, u32[]{:S(2)}) collective-permute-start(bf16[16,4096]{1,0:T(8,128)(2,1)S(1)} %get-tuple-element.611), channel_id=1, source_target_pairs={{16,0},{32,16},{48,32},{64,48},{80,64},{96,80},{112,96},{128,112},... | collective-permute-start | bytes 393224 | tf_op jit(solution)/shard_map/while/body/eval_jaxpr/ppermute | solution.py:12
  685.4 12.3 %collective-permute-start = (bf16[16,4096]{1,0:T(8,128)(2,1)S(1)}, bf16[16,4096]{1,0:T(8,128)(2,1)S(1)}, u32[]{:S(2)}, u32[]{:S(2)}) collective-permute-start(bf16[16,4096]{1,0:T(8,128)(2,1)S(1)} %get-tuple-element.611), channel_id=1, source_target_pairs={{16,0},{32,16},{48,32},{64,48},{80,64},{96,80},{112,96},{128,112},... | collective-permute-start | bytes 393224 | tf_op jit(solution)/shard_map/while/body/eval_jaxpr/ppermute | solution.py:12
  697.7 12.3 %collective-permute-start = (bf16[16,4096]{1,0:T(8,128)(2,1)S(1)}, bf16[16,4096]{1,0:T(8,128)(2,1)S(1)}, u32[]{:S(2)}, u32[]{:S(2)}) collective-permute-start(bf16[16,4096]{1,0:T(8,128)(2,1)S(1)} %get-tuple-element.611), channel_id=1, source_target_pairs={{16,0},{32,16},{48,32},{64,48},{80,64},{96,80},{112,96},{128,112},... | collective-permute-start | bytes 393224 | tf_op jit(solution)/shard_map/while/body/eval_jaxpr/ppermute | solution.py:12
  710.0 12.3 %collective-permute-start = (bf16[16,4096]{1,0:T(8,128)(2,1)S(1)}, bf16[16,4096]{1,0:T(8,128)(2,1)S(1)}, u32[]{:S(2)}, u32[]{:S(2)}) collective-permute-start(bf16[16,4096]{1,0:T(8,128)(2,1)S(1)} %get-tuple-element.611), channel_id=1, source_target_pairs={{16,0},{32,16},{48,32},{64,48},{80,64},{96,80},{112,96},{128,112},... | collective-permute-start | bytes 393224 | tf_op jit(solution)/shard_map/while/body/eval_jaxpr/ppermute | solution.py:12
  722.4 12.3 %collective-permute-start = (bf16[16,4096]{1,0:T(8,128)(2,1)S(1)}, bf16[16,4096]{1,0:T(8,128)(2,1)S(1)}, u32[]{:S(2)}, u32[]{:S(2)}) collective-permute-start(bf16[16,4096]{1,0:T(8,128)(2,1)S(1)} %get-tuple-element.611), channel_id=1, source_target_pairs={{16,0},{32,16},{48,32},{64,48},{80,64},{96,80},{112,96},{128,112},... | collective-permute-start | bytes 393224 | tf_op jit(solution)/shard_map/while/body/eval_jaxpr/ppermute | solution.py:12
  734.7 12.3 %collective-permute-start = (bf16[16,4096]{1,0:T(8,128)(2,1)S(1)}, bf16[16,4096]{1,0:T(8,128)(2,1)S(1)}, u32[]{:S(2)}, u32[]{:S(2)}) collective-permute-start(bf16[16,4096]{1,0:T(8,128)(2,1)S(1)} %get-tuple-element.611), channel_id=1, source_target_pairs={{16,0},{32,16},{48,32},{64,48},{80,64},{96,80},{112,96},{128,112},... | collective-permute-start | bytes 393224 | tf_op jit(solution)/shard_map/while/body/eval_jaxpr/ppermute | solution.py:12
  747.0 12.3 %collective-permute-start = (bf16[16,4096]{1,0:T(8,128)(2,1)S(1)}, bf16[16,4096]{1,0:T(8,128)(2,1)S(1)}, u32[]{:S(2)}, u32[]{:S(2)}) collective-permute-start(bf16[16,4096]{1,0:T(8,128)(2,1)S(1)} %get-tuple-element.611), channel_id=1, source_target_pairs={{16,0},{32,16},{48,32},{64,48},{80,64},{96,80},{112,96},{128,112},... | collective-permute-start | bytes 393224 | tf_op jit(solution)/shard_map/while/body/eval_jaxpr/ppermute | solution.py:12
  759.4 12.3 %collective-permute-start = (bf16[16,4096]{1,0:T(8,128)(2,1)S(1)}, bf16[16,4096]{1,0:T(8,128)(2,1)S(1)}, u32[]{:S(2)}, u32[]{:S(2)}) collective-permute-start(bf16[16,4096]{1,0:T(8,128)(2,1)S(1)} %get-tuple-element.611), channel_id=1, source_target_pairs={{16,0},{32,16},{48,32},{64,48},{80,64},{96,80},{112,96},{128,112},... | collective-permute-start | bytes 393224 | tf_op jit(solution)/shard_map/while/body/eval_jaxpr/ppermute | solution.py:12
  771.7 12.3 %collective-permute-start = (bf16[16,4096]{1,0:T(8,128)(2,1)S(1)}, bf16[16,4096]{1,0:T(8,128)(2,1)S(1)}, u32[]{:S(2)}, u32[]{:S(2)}) collective-permute-start(bf16[16,4096]{1,0:T(8,128)(2,1)S(1)} %get-tuple-element.611), channel_id=1, source_target_pairs={{16,0},{32,16},{48,32},{64,48},{80,64},{96,80},{112,96},{128,112},... | collective-permute-start | bytes 393224 | tf_op jit(solution)/shard_map/while/body/eval_jaxpr/ppermute | solution.py:12
  784.0 12.3 %collective-permute-start = (bf16[16,4096]{1,0:T(8,128)(2,1)S(1)}, bf16[16,4096]{1,0:T(8,128)(2,1)S(1)}, u32[]{:S(2)}, u32[]{:S(2)}) collective-permute-start(bf16[16,4096]{1,0:T(8,128)(2,1)S(1)} %get-tuple-element.611), channel_id=1, source_target_pairs={{16,0},{32,16},{48,32},{64,48},{80,64},{96,80},{112,96},{128,112},... | collective-permute-start | bytes 393224 | tf_op jit(solution)/shard_map/while/body/eval_jaxpr/ppermute | solution.py:12
  799.1 1.2 copy-start.4
Sparse Core Ops, SparseCore 0:
  10.1 88.6 all-gather.10
  100.9 83.6 all-gather.6
  186.5 85.0 all-gather.12
  274.2 83.3 all-gather.8
  799.3 124.8 reduce-scatter.1
where the time goes:
time: 935 us; the launch traced here: 932 us
  waiting for transfers between devices  714 us (76%)
  starting transfers between devices  87.2 us (9%)
  blocking collectives  43.8 us (5%)
  other arithmetic  33.4 us (4%)
  matrix products  32.9 us (4%)
  between operations  13.8 us (1%)
    ppermute x39, waiting for transfers between devices, from_behind(): return lax.ppermute(block, axis, route)  379 us
    all_gather x1, waiting for transfers between devices, per_device(): lax.all_gather(up_proj[0], 'dp', axis=1, tiled=True)  87.1 us
    ppermute x39, starting transfers between devices, from_behind(): return lax.ppermute(block, axis, route)  87 us
    all_gather x1, waiting for transfers between devices, per_device(): lax.all_gather(down_proj[0], 'dp', axis=0, tiled=True)  87 us
    all_gather x1, waiting for transfers between devices, per_device(): lax.all_gather(readout_matrix, 'dp', axis=0, tiled=True)  80.8 us
    reduce_scatter x1, waiting for transfers between devices, per_device(): lax.psum_scatter(contract_rows(normed, latent_grads), 'dp', scatter_dimen...  77.1 us
    all_to_all x1, blocking collectives, per_device(): lax.all_to_all(cotangents, 'dp', split_axis=1, concat_axis=0, tiled=True)  43.8 us
    dot_general x16, matrix products, multiply_trailing_factor(): lax.dot_general(left, right, (((1,), (1,)), ((), ())), preferred_element_...  24.7 us
  transfers between devices with their start and end apart: 44, of which 43 were waited for; matrix products, arithmetic and copies ran while one was open for 7% of the time, Pallas kernels for 0%

commit v1 on v0

v1 whole, which is shorter than its diff:
```python
import functools

import jax
import jax.numpy as jnp
from jax import lax
from jax.experimental import pallas as pl
from jax.experimental.pallas import tpu as pltpu
from jax.sharding import PartitionSpec as P

EPSILON = 1e-05
MESH = pl.DeviceIdType.MESH
F32 = jnp.float32
BF16 = jnp.bfloat16
LINE = 4


def matmul(left, right):
    return jnp.dot(left, right, preferred_element_type=F32)


def matmul_nt(left, right):
    return lax.dot_general(left, right, (((1,), (1,)), ((), ())), preferred_element_type=F32)


def matmul_tn(left, right):
    return lax.dot_general(left, right, (((0,), (0,)), ((), ())), preferred_element_type=F32)


def copy_to(src, dst, send, recv, dev):
    return pltpu.make_async_remote_copy(
        src_ref=src, dst_ref=dst, send_sem=send, recv_sem=recv, device_id=dev, device_id_type=MESH
    )


def kernel(
    ndp,
    nsec,
    x_ref,
    gain_ref,
    down_ref,
    up_ref,
    ro_ref,
    gt_ref,
    vl_ref,
    out_ref,
    dg_ref,
    ug_ref,
    wd,
    wu,
    ro,
    normed,
    ncols,
    act,
    lat,
    dsil,
    inv,
    inc,
    lg,
    cot,
    outp,
    w_send,
    w_recv,
    ro_send,
    ro_recv,
    n_send,
    n_recv,
    a_send,
    a_recv,
    c_send,
    c_recv,
    l_send,
    l_recv,
    r_send,
    r_recv,
    own_sem,
):
    nmb, rows, width = inc.shape
    ntok = nmb * rows
    blk = wd.shape[1]
    latw = wd.shape[2]
    sec = lax.axis_index("section")
    me = lax.axis_index("dp")
    ncol = ndp // LINE
    mx = me // LINE
    my = me % LINE
    last = nsec - 1

    def at(xx, yy):
        return {"dp": (xx % ncol) * LINE + yy % LINE}

    def peer(j):
        return (me + j) % ndp

    barrier = pltpu.get_barrier_semaphore()

    def greet(j, c):
        pl.semaphore_signal(barrier, inc=1, device_id={"dp": peer(j)}, device_id_type=MESH)
        return c

    lax.fori_loop(1, ndp, greet, 0)

    @pl.when(sec > 0)
    def _():
        pl.semaphore_signal(barrier, inc=1, device_id={"section": sec - 1}, device_id_type=MESH)

    @pl.when(sec < last)
    def _():
        pl.semaphore_signal(barrier, inc=1, device_id={"section": sec + 1}, device_id_type=MESH)

    wd[me] = down_ref[...].T
    wu[me] = up_ref[...].T
    ro[me] = ro_ref[...]

    @pl.when((sec > 0) & (sec < last))
    def _():
        pl.semaphore_wait(barrier, ndp + 1)

    @pl.when((sec == 0) | (sec == last))
    def _():
        pl.semaphore_wait(barrier, ndp)

    pieces = (wd, wu)

    def send_block(e, k, dev):
        copy_to(pieces[k].at[e], pieces[k].at[e], w_send, w_recv.at[k, e], dev).start()

    def wait_block(e, k):
        copy_to(pieces[k].at[e], pieces[k].at[e], w_send, w_recv.at[k, e], at(mx, my)).wait_recv()

    for k in (0, 1):
        send_block(me, k, at(mx + 1, my))
        send_block(me, k, at(mx + ncol - 1, my))
        for j in range(1, LINE):
            send_block(me, k, at(mx, my + j))

    @pl.when(sec == last)
    def _():
        def send_ro(j, c):
            copy_to(ro.at[me], ro.at[me], ro_send, ro_recv, {"dp": peer(j)}).start()
            return c

        lax.fori_loop(1, ndp, send_ro, 0)

    gain = gain_ref[...].astype(F32)
    values = x_ref[...].astype(F32)
    inverse = lax.rsqrt(jnp.mean(values * values, axis=-1, keepdims=True) + EPSILON)
    inv[...] = jnp.broadcast_to(inverse, inv.shape)
    for b in range(ndp):
        cols = slice(b * blk, (b + 1) * blk)
        unit = x_ref[:, cols].astype(F32) * inverse
        normed[b] = (unit * gain[:, cols]).astype(BF16)

    for j in range(1, LINE):
        e = mx * LINE + (my + j) % LINE
        for k in (0, 1):
            wait_block(e, k)
            send_block(e, k, at(mx + 1, my))
            send_block(e, k, at(mx + ncol - 1, my))
    for j in range(LINE):
        e_left = ((mx + ncol - 1) % ncol) * LINE + (my + j) % LINE
        e_right = ((mx + 1) % ncol) * LINE + (my + j) % LINE
        wait_block(e_left, 0)
        send_block(e_left, 0, at(mx + 1, my))
        wait_block(e_right, 1)
        send_block(e_right, 1, at(mx + ncol - 1, my))
    for j in range(LINE):
        e_left = ((mx + ncol - 1) % ncol) * LINE + (my + j) % LINE
        e_right = ((mx + 1) % ncol) * LINE + (my + j) % LINE
        e_far = ((mx + 2) % ncol) * LINE + (my + j) % LINE
        wait_block(e_left, 1)
        wait_block(e_right, 0)
        wait_block(e_far, 0)
        wait_block(e_far, 1)

    def latent_step(b, acc):
        return acc + matmul_nt(normed[b], wd[b])

    latent = lax.fori_loop(0, ndp, latent_step, jnp.zeros((ntok, latw), F32))
    lat[...] = latent
    sigmoid = jax.nn.sigmoid(latent)
    activated = (latent * sigmoid).astype(BF16)
    act[me] = activated
    dsil[...] = sigmoid * (1.0 + latent * (1.0 - sigmoid))

    @pl.when(sec == last)
    def _():
        copy_to(ro.at[pl.ds(0, ndp - 1)], ro.at[pl.ds(0, ndp - 1)], ro_send, ro_recv, at(mx, my)).wait_recv()
        hidden = act[me]
        est = jnp.zeros((ntok, ro.shape[2]), F32)
        for b in range(ndp):
            cols = slice(b * blk, (b + 1) * blk)
            adapter = x_ref[:, cols].astype(F32) + matmul_nt(hidden, wu[b])
            est = est + matmul(adapter.astype(BF16), ro[b])
        diff = est - gt_ref[...]
        offset = lax.broadcasted_iota(jnp.int32, (rows, diff.shape[1]), 0)
        errs = []
        for m in range(nmb):
            mask = jnp.where(offset < vl_ref[m], 1.0, 0.0)
            errs.append(mask * diff[m * rows : (m + 1) * rows])
        error = jnp.concatenate(errs, axis=0).astype(BF16)
        for b in range(ndp):
            cols = slice(b * blk, (b + 1) * blk)
            top = matmul_nt(error, ro[b]).astype(BF16)
            inc[:, :, cols] = top.reshape(nmb, rows, blk)

    def send_early(j, c):
        p = peer(j)
        copy_to(act.at[me], act.at[me], a_send, a_recv, {"dp": p}).start()
        copy_to(normed.at[p], ncols.at[me], n_send, n_recv, {"dp": p}).start()
        return c

    lax.fori_loop(1, ndp, send_early, 0)
    ncols[me] = normed[me]

    def relay_copy(m):
        return copy_to(outp.at[m], inc.at[m], r_send.at[m], r_recv.at[m], {"section": (sec + last) % nsec})

    def step(m, c):
        @pl.when(sec < last)
        def _():
            relay_copy(m).wait_recv()

        tok = pl.ds(pl.multiple_of(m * rows, rows), rows)
        h = jnp.zeros((rows, latw), F32)
        for b in range(ndp):
            h = h + matmul(inc[m, :, b * blk : (b + 1) * blk], wu[b])
        latent_grad = (h * dsil[tok, :]).astype(BF16)
        lg[me, m] = latent_grad
        iv = inv[tok, 0:1]
        mean = jnp.sum(latent_grad.astype(F32) * lat[tok, :], axis=-1, keepdims=True) * (1.0 / width)
        for b in range(ndp):
            cols = slice(b * blk, (b + 1) * blk)
            scaled = matmul(latent_grad, wd[b]) * gain_ref[:, cols].astype(F32)
            unit = x_ref[tok, cols].astype(F32) * iv
            g = inc[m, :, cols].astype(F32) + iv * (scaled - unit * mean)
            outp[m, :, cols] = g.astype(BF16)

        @pl.when(sec > 0)
        def _():
            relay_copy(m).start()

        return c

    half = nmb // 2
    own_cols = pl.ds(pl.multiple_of(me * blk, blk), blk)
    for lo, hi in ((0, half), (half, nmb)):
        lax.fori_loop(lo, hi, step, 0)
        part = pl.ds(lo, hi - lo)

        def send_late(j, c, part=part):
            p = peer(j)
            p_cols = pl.ds(pl.multiple_of(p * blk, blk), blk)
            copy_to(inc.at[part, :, p_cols], cot.at[me, part], c_send, c_recv, {"dp": p}).start()
            copy_to(lg.at[me, part], lg.at[me, part], l_send, l_recv, {"dp": p}).start()
            return c

        lax.fori_loop(1, ndp, send_late, 0)
    own = pltpu.make_async_copy(inc.at[:, :, own_cols], cot.at[me], own_sem)
    own.start()
    out_ref[...] = outp[...].reshape(ntok, width)
    own.wait()

    others = pl.ds(0, ndp - 1)
    copy_to(act.at[others], act.at[others], a_send, a_recv, at(mx, my)).wait_recv()
    copy_to(ncols.at[others], ncols.at[others], n_send, n_recv, at(mx, my)).wait_recv()
    copy_to(cot.at[others], cot.at[others], c_send, c_recv, at(mx, my)).wait_recv()
    copy_to(lg.at[others], lg.at[others], l_send, l_recv, at(mx, my)).wait_recv()
    ug = matmul_tn(act[...].reshape(ndp * ntok, latw), cot[...].reshape(ndp * ntok, blk))
    ug_ref[...] = ug.astype(BF16)
    dg = matmul_tn(ncols[...].reshape(ndp * ntok, blk), lg[...].reshape(ndp * ntok, latw))
    dg_ref[...] = dg.astype(BF16)

    for k in (0, 1):
        copy_to(pieces[k].at[others], pieces[k].at[others], w_send, w_recv.at[k, 0], at(mx, my)).wait_send()

    @pl.when(sec == last)
    def _():
        copy_to(ro.at[others], ro.at[others], ro_send, ro_recv, at(mx, my)).wait_send()

    copy_to(act.at[others], act.at[others], a_send, a_recv, at(mx, my)).wait_send()
    copy_to(ncols.at[others], ncols.at[others], n_send, n_recv, at(mx, my)).wait_send()
    copy_to(cot.at[others], cot.at[others], c_send, c_recv, at(mx, my)).wait_send()
    copy_to(lg.at[others], lg.at[others], l_send, l_recv, at(mx, my)).wait_send()

    @pl.when(sec > 0)
    def _():
        def left(m, c):
            relay_copy(m).wait_send()
            return c

        lax.fori_loop(0, nmb, left, 0)


def per_device(
    ndp, nsec, section_inputs, norm_gain, down_proj, up_proj, readout_matrix, ground_truth_series, valid_len
):
    _, ntok, width = section_inputs.shape
    _, blk, latw = down_proj.shape
    horizon = readout_matrix.shape[1]
    nmb = valid_len.shape[0]
    rows = ntok // nmb
    vmem = pl.BlockSpec(memory_space=pltpu.VMEM)
    dma = pltpu.SemaphoreType.DMA
    grads, dg, ug = pl.pallas_call(
        functools.partial(kernel, ndp, nsec),
        name="relay",
        out_shape=(
            jax.ShapeDtypeStruct((ntok, width), BF16),
            jax.ShapeDtypeStruct((blk, latw), BF16),
            jax.ShapeDtypeStruct((latw, blk), BF16),
        ),
        in_specs=[vmem] * 6 + [pl.BlockSpec(memory_space=pltpu.SMEM)],
        out_specs=(vmem, vmem, vmem),
        scratch_shapes=[
            pltpu.VMEM((ndp, latw, blk), BF16),
            pltpu.VMEM((ndp, blk, latw), BF16),
            pltpu.VMEM((ndp, blk, horizon), BF16),
            pltpu.VMEM((ndp, ntok, blk), BF16),
            pltpu.VMEM((ndp, ntok, blk), BF16),
            pltpu.VMEM((ndp, ntok, latw), BF16),
            pltpu.VMEM((ntok, latw), F32),
            pltpu.VMEM((ntok, latw), F32),
            pltpu.VMEM((ntok, 128), F32),
            pltpu.VMEM((nmb, rows, width), BF16),
            pltpu.VMEM((ndp, nmb, rows, latw), BF16),
            pltpu.VMEM((ndp, nmb, rows, blk), BF16),
            pltpu.VMEM((nmb, rows, width), BF16),
            dma,
            dma((2, ndp)),
            dma,
            dma,
            dma,
            dma,
            dma,
            dma,
            dma,
            dma,
            dma,
            dma,
            dma((nmb,)),
            dma((nmb,)),
            dma,
        ],
        compiler_params=pltpu.CompilerParams(collective_id=0, has_side_effects=True),
    )(
        section_inputs[0],
        norm_gain,
        down_proj[0],
        up_proj[0],
        readout_matrix,
        ground_truth_series,
        valid_len,
    )
    return grads[None], dg[None], ug[None]


def solution(mesh):
    placed = (
        P("section", "dp", None),
        P("section", None),
        P("section", "dp", None),
        P("section", None, "dp"),
        P("dp", None),
        P("dp", None),
        P("dp"),
    )
    return jax.shard_map(
        functools.partial(per_device, mesh.shape["dp"], mesh.shape["section"]),
        mesh=mesh,
        in_specs=placed,
        out_specs=(P("section", "dp", None), P("section", "dp", None), P("section", None, "dp")),
        check_vma=False,
    )
```

time: 935 us -> 260 us (0.28)
  the two profiles are of different devices: /device:TPU:448 before, /device:TPU:28 now
where the time goes in v1:
time: 260 us
  Pallas kernels  256 us (98%)
  local copies, waits for them, and re-layouts  3.93 us (2%)
    pallas_call x1, Pallas kernels, per_device(): pl.pallas_call(functools.partial(kernel, ndp, nsec), name='relay', out_sh...  256 us

profile of v1, /device:TPU:28, one launch (start us, length us, event | category | flops | bytes accessed | tf_op | source)
XLA Modules:
  0.0 260.1 jit_solution(18113763529736971393)
XLA Ops:
  0.6 255.5 %relay.1 = (bf16[128,4096]{1,0:T(8,128)(2,1)}, bf16[256,256]{1,0:T(8,128)(2,1)}, bf16[256,256]{1,0:T(8,128)(2,1)}) custom-call(bf16[128,4096]{1,0:T(8,128)(2,1)} %bitcast.6, bf16[1,4096]{1,0:T(2,128)(2,1)} %gain_ref.1, bf16[256,256]{1,0:T(8,128)(2,1)} %bitcast.10, bf16[256,256]{1,0:T(8,128)(2,1)} %bitcast.11, bf16[256,128]{1,0:T(8,128)(2,1)} %ro_ref.1, ...), custom_call_target="tpu_custom_call" | custom-call | tf_op jit(solution)/shard_map/relay/pallas_call | solution.py:304
  256.2 0.0 copy-start.1
  256.2 2.3 copy.13
  258.5 0.0 copy-done.1
  258.5 0.0 copy-start
  258.5 0.7 copy.14
  259.2 0.3 copy-done
  259.5 0.7 copy.15
Async XLA Ops:
  256.2 2.3 copy-start.1
  258.5 1.0 copy-start

commit v2 on v1

--- a/solution.py
+++ b/solution.py
@@ -12,6 +12,10 @@
 F32 = jnp.float32
 BF16 = jnp.bfloat16
 LINE = 4
+GROUP = 2
+TOP = 8
+SPLIT = 4
+COT_GROUPS = 2
 
 
 def matmul(left, right):
@@ -73,6 +77,7 @@
     r_send,
     r_recv,
     own_sem,
+    clear,
 ):
     nmb, rows, width = inc.shape
     ntok = nmb * rows
@@ -127,11 +132,20 @@
     def wait_block(e, k):
         copy_to(pieces[k].at[e], pieces[k].at[e], w_send, w_recv.at[k, e], at(mx, my)).wait_recv()
 
+    left, right = at(mx + ncol - 1, my), at(mx + 1, my)
+    order = (my, 1 + my % 2, (my * 3 + 2) % 5, 3 * (1 - my // 2))
+
+    def column(shift, row):
+        return ((mx + shift + ncol) % ncol) * LINE + row
+
+    even = sec % 2 == 0
+
+
     for k in (0, 1):
-        send_block(me, k, at(mx + 1, my))
-        send_block(me, k, at(mx + ncol - 1, my))
-        for j in range(1, LINE):
-            send_block(me, k, at(mx, my + j))
+        send_block(me, k, left)
+        send_block(me, k, right)
+        for row in order[1:]:
+            send_block(me, k, at(mx, row))
 
     @pl.when(sec == last)
     def _():
@@ -150,27 +164,25 @@
         unit = x_ref[:, cols].astype(F32) * inverse
         normed[b] = (unit * gain[:, cols]).astype(BF16)
 
-    for j in range(1, LINE):
-        e = mx * LINE + (my + j) % LINE
-        for k in (0, 1):
-            wait_block(e, k)
-            send_block(e, k, at(mx + 1, my))
-            send_block(e, k, at(mx + ncol - 1, my))
-    for j in range(LINE):
-        e_left = ((mx + ncol - 1) % ncol) * LINE + (my + j) % LINE
-        e_right = ((mx + 1) % ncol) * LINE + (my + j) % LINE
-        wait_block(e_left, 0)
-        send_block(e_left, 0, at(mx + 1, my))
-        wait_block(e_right, 1)
-        send_block(e_right, 1, at(mx + ncol - 1, my))
-    for j in range(LINE):
-        e_left = ((mx + ncol - 1) % ncol) * LINE + (my + j) % LINE
-        e_right = ((mx + 1) % ncol) * LINE + (my + j) % LINE
-        e_far = ((mx + 2) % ncol) * LINE + (my + j) % LINE
-        wait_block(e_left, 1)
-        wait_block(e_right, 0)
-        wait_block(e_far, 0)
-        wait_block(e_far, 1)
+    for i in range(1, LINE + 1):
+        if i < LINE:
+            for k in (0, 1):
+                e = column(0, order[i])
+                wait_block(e, k)
+                send_block(e, k, left)
+                send_block(e, k, right)
+        e = column(-1, order[i - 1])
+        wait_block(e, 0)
+        send_block(e, 0, right)
+        e = column(1, order[i - 1])
+        wait_block(e, 1)
+        send_block(e, 1, left)
+    for row in order:
+        wait_block(column(-1, row), 1)
+        wait_block(column(1, row), 0)
+        wait_block(column(2, row), 0)
+        wait_block(column(2, row), 1)
+
 
     def latent_step(b, acc):
         return acc + matmul_nt(normed[b], wd[b])
@@ -209,52 +221,115 @@
         copy_to(normed.at[p], ncols.at[me], n_send, n_recv, {"dp": p}).start()
         return c
 
-    lax.fori_loop(1, ndp, send_early, 0)
+    @pl.when(even & (sec < nsec - TOP))
+    def _():
+        pl.semaphore_signal(clear, inc=1, device_id={"section": sec + 1}, device_id_type=MESH)
+
+    @pl.when(jnp.logical_not(even) & (sec < nsec - TOP))
+    def _():
+        pl.semaphore_wait(clear, 1)
+
+    @pl.when(sec < nsec - TOP)
+    def _():
+        lax.fori_loop(1, ndp, send_early, 0)
+
     ncols[me] = normed[me]
 
-    def relay_copy(m):
-        return copy_to(outp.at[m], inc.at[m], r_send.at[m], r_recv.at[m], {"section": (sec + last) % nsec})
+    below = {"section": (sec + last) % nsec}
+    per = ndp // SPLIT
+
+    def relay_copy(m, q):
+        cols = slice(q * per * blk, (q + 1) * per * blk)
+        return copy_to(outp.at[m, :, cols], inc.at[m, :, cols], r_send.at[m, q], r_recv.at[m, q], below)
 
     def step(m, c):
-        @pl.when(sec < last)
-        def _():
-            relay_copy(m).wait_recv()
-
         tok = pl.ds(pl.multiple_of(m * rows, rows), rows)
         h = jnp.zeros((rows, latw), F32)
-        for b in range(ndp):
-            h = h + matmul(inc[m, :, b * blk : (b + 1) * blk], wu[b])
+        for q in range(SPLIT):
+
+            @pl.when(sec < last)
+            def _(q=q):
+                relay_copy(m, q).wait_recv()
+
+            for b in range(q * per, (q + 1) * per):
+                h = h + matmul(inc[m, :, b * blk : (b + 1) * blk], wu[b])
         latent_grad = (h * dsil[tok, :]).astype(BF16)
         lg[me, m] = latent_grad
         iv = inv[tok, 0:1]
         mean = jnp.sum(latent_grad.astype(F32) * lat[tok, :], axis=-1, keepdims=True) * (1.0 / width)
-        for b in range(ndp):
-            cols = slice(b * blk, (b + 1) * blk)
-            scaled = matmul(latent_grad, wd[b]) * gain_ref[:, cols].astype(F32)
-            unit = x_ref[tok, cols].astype(F32) * iv
-            g = inc[m, :, cols].astype(F32) + iv * (scaled - unit * mean)
-            outp[m, :, cols] = g.astype(BF16)
-
-        @pl.when(sec > 0)
+        for q in range(SPLIT):
+            for b in range(q * per, (q + 1) * per):
+                cols = slice(b * blk, (b + 1) * blk)
+                scaled = matmul(latent_grad, wd[b]) * gain_ref[:, cols].astype(F32)
+                unit = x_ref[tok, cols].astype(F32) * iv
+                g = inc[m, :, cols].astype(F32) + iv * (scaled - unit * mean)
+                outp[m, :, cols] = g.astype(BF16)
+
+            @pl.when(sec > 0)
+            def _(q=q):
+                relay_copy(m, q).start()
+
+        return c
+
+    own_cols = pl.ds(pl.multiple_of(me * blk, blk), blk)
+
+    def send_lg(e, g, dev):
+        part = pl.ds(g * GROUP, GROUP)
+        copy_to(lg.at[e, part], lg.at[e, part], l_send, l_recv.at[e, g], dev).start()
+
+    def wait_lg(e, g):
+        part = pl.ds(g * GROUP, GROUP)
+        copy_to(lg.at[e, part], lg.at[e, part], l_send, l_recv.at[e, g], left).wait_recv()
+
+    def pass_on(g):
+        @pl.when(g < groups)
         def _():
-            relay_copy(m).start()
-
+            send_lg(me, g, left)
+            send_lg(me, g, right)
+            for row in order[1:]:
+                send_lg(me, g, at(mx, row))
+        @pl.when((g < groups) & (g % COT_GROUPS == COT_GROUPS - 1))
+        def _():
+            part = pl.ds((g + 1 - COT_GROUPS) * GROUP, GROUP * COT_GROUPS)
+
+            def send_cot(j, c):
+                p = peer(j)
+                p_cols = pl.ds(pl.multiple_of(p * blk, blk), blk)
+                copy_to(inc.at[part, :, p_cols], cot.at[me, part], c_send, c_recv, {"dp": p}).start()
+                return c
+
+            lax.fori_loop(1, ndp, send_cot, 0)
+
+        @pl.when((g >= 1) & (g <= groups))
+        def _():
+            for row in order[1:]:
+                wait_lg(column(0, row), g - 1)
+                send_lg(column(0, row), g - 1, left)
+                send_lg(column(0, row), g - 1, right)
+
+        @pl.when(g >= 2)
+        def _():
+            for n, row in enumerate(order):
+                near = 1 if n % 2 else -1
+                e = column(near, row)
+                wait_lg(e, g - 2)
+                send_lg(e, g - 2, left if n % 2 else right)
+
+    groups = nmb // GROUP
+
+    def stretch(g, c):
+        lax.fori_loop(g * GROUP, (g + 1) * GROUP, step, 0)
+        pass_on(g)
         return c
 
-    half = nmb // 2
-    own_cols = pl.ds(pl.multiple_of(me * blk, blk), blk)
-    for lo, hi in ((0, half), (half, nmb)):
-        lax.fori_loop(lo, hi, step, 0)
-        part = pl.ds(lo, hi - lo)
-
-        def send_late(j, c, part=part):
-            p = peer(j)
-            p_cols = pl.ds(pl.multiple_of(p * blk, blk), blk)
-            copy_to(inc.at[part, :, p_cols], cot.at[me, part], c_send, c_recv, {"dp": p}).start()
-            copy_to(lg.at[me, part], lg.at[me, part], l_send, l_recv, {"dp": p}).start()
-            return c
-
-        lax.fori_loop(1, ndp, send_late, 0)
+    lax.fori_loop(0, groups, stretch, 0)
+    pass_on(groups)
+    pass_on(groups + 1)
+
+    @pl.when(sec >= nsec - TOP)
+    def _():
+        lax.fori_loop(1, ndp, send_early, 0)
+
     own = pltpu.make_async_copy(inc.at[:, :, own_cols], cot.at[me], own_sem)
     own.start()
     out_ref[...] = outp[...].reshape(ntok, width)
@@ -264,7 +339,14 @@
     copy_to(act.at[others], act.at[others], a_send, a_recv, at(mx, my)).wait_recv()
     copy_to(ncols.at[others], ncols.at[others], n_send, n_recv, at(mx, my)).wait_recv()
     copy_to(cot.at[others], cot.at[others], c_send, c_recv, at(mx, my)).wait_recv()
-    copy_to(lg.at[others], lg.at[others], l_send, l_recv, at(mx, my)).wait_recv()
+
+    def last_lg(g, c):
+        for n, row in enumerate(order):
+            wait_lg(column(-1 if n % 2 else 1, row), g)
+            wait_lg(column(2, row), g)
+        return c
+
+    lax.fori_loop(0, groups, last_lg, 0)
     ug = matmul_tn(act[...].reshape(ndp * ntok, latw), cot[...].reshape(ndp * ntok, blk))
     ug_ref[...] = ug.astype(BF16)
     dg = matmul_tn(ncols[...].reshape(ndp * ntok, blk), lg[...].reshape(ndp * ntok, latw))
@@ -280,15 +362,16 @@
     copy_to(act.at[others], act.at[others], a_send, a_recv, at(mx, my)).wait_send()
     copy_to(ncols.at[others], ncols.at[others], n_send, n_recv, at(mx, my)).wait_send()
     copy_to(cot.at[others], cot.at[others], c_send, c_recv, at(mx, my)).wait_send()
-    copy_to(lg.at[others], lg.at[others], l_send, l_recv, at(mx, my)).wait_send()
+    copy_to(lg.at[others], lg.at[others], l_send, l_recv.at[0, 0], left).wait_send()
 
     @pl.when(sec > 0)
     def _():
-        def left(m, c):
-            relay_copy(m).wait_send()
+        def gone(m, c):
+            for q in range(SPLIT):
+                relay_copy(m, q).wait_send()
             return c
 
-        lax.fori_loop(0, nmb, left, 0)
+        lax.fori_loop(0, nmb, gone, 0)
 
 
 def per_device(
@@ -336,10 +419,11 @@
             dma,
             dma,
             dma,
-            dma,
-            dma((nmb,)),
-            dma((nmb,)),
-            dma,
+            dma((ndp, nmb // GROUP)),
+            dma((nmb, SPLIT)),
+            dma((nmb, SPLIT)),
+            dma,
+            pltpu.SemaphoreType.REGULAR,
         ],
         compiler_params=pltpu.CompilerParams(collective_id=0, has_side_effects=True),
     )(

time: 260 us -> 233 us (0.90)
  the two profiles are of different devices: /device:TPU:28 before, /device:TPU:2 now
where the time goes in v2:
time: 233 us
  Pallas kernels  228 us (98%)
  local copies, waits for them, and re-layouts  3.93 us (2%)
    pallas_call x1, Pallas kernels, per_device(): pl.pallas_call(functools.partial(kernel, ndp, nsec), name='relay', out_sh...  228 us

profile of v2, /device:TPU:2, one launch (start us, length us, event | category | flops | bytes accessed | tf_op | source)
XLA Modules:
  0.0 233.0 jit_solution(17082475552512586633)
XLA Ops:
  0.6 228.4 %relay.1 = (bf16[128,4096]{1,0:T(8,128)(2,1)}, bf16[256,256]{1,0:T(8,128)(2,1)}, bf16[256,256]{1,0:T(8,128)(2,1)}) custom-call(bf16[128,4096]{1,0:T(8,128)(2,1)} %bitcast.6, bf16[1,4096]{1,0:T(2,128)(2,1)} %gain_ref.1, bf16[256,256]{1,0:T(8,128)(2,1)} %bitcast.10, bf16[256,256]{1,0:T(8,128)(2,1)} %bitcast.11, bf16[256,128]{1,0:T(8,128)(2,1)} %ro_ref.1, ...), custom_call_target="tpu_custom_call" | custom-call | tf_op jit(solution)/shard_map/relay/pallas_call | solution.py:387
  229.0 0.0 copy-start.1
  229.0 2.3 copy.13
  231.4 0.0 copy-done.1
  231.4 0.0 copy-start
  231.4 0.7 copy.14
  232.0 0.3 copy-done
  232.3 0.7 copy.15
Async XLA Ops:
  229.0 2.3 %copy-start.1 = (bf16[256,256]{1,0:T(8,128)(2,1)S(1)}, bf16[256,256]{1,0:T(8,128)(2,1)}, u32[]{:S(2)}) copy-start(bf16[256,256]{1,0:T(8,128)(2,1)} %get-tuple-element.7) | copy-start | bytes 393220
  231.4 1.0 copy-start

commit v3 on v2

--- a/solution.py
+++ b/solution.py
@@ -62,6 +62,7 @@
     lg,
     cot,
     outp,
+    est,
     w_send,
     w_recv,
     ro_send,
@@ -77,6 +78,7 @@
     r_send,
     r_recv,
     own_sem,
+    out_sem,
     clear,
 ):
     nmb, rows, width = inc.shape
@@ -164,25 +166,19 @@
         unit = x_ref[:, cols].astype(F32) * inverse
         normed[b] = (unit * gain[:, cols]).astype(BF16)
 
-    for i in range(1, LINE + 1):
-        if i < LINE:
-            for k in (0, 1):
+    for k, near, way in ((0, -1, right), (1, 1, left)):
+        for i in range(1, LINE + 1):
+            if i < LINE:
                 e = column(0, order[i])
                 wait_block(e, k)
                 send_block(e, k, left)
                 send_block(e, k, right)
-        e = column(-1, order[i - 1])
-        wait_block(e, 0)
-        send_block(e, 0, right)
-        e = column(1, order[i - 1])
-        wait_block(e, 1)
-        send_block(e, 1, left)
+            e = column(near, order[i - 1])
+            wait_block(e, k)
+            send_block(e, k, way)
     for row in order:
-        wait_block(column(-1, row), 1)
         wait_block(column(1, row), 0)
         wait_block(column(2, row), 0)
-        wait_block(column(2, row), 1)
-
 
     def latent_step(b, acc):
         return acc + matmul_nt(normed[b], wd[b])
@@ -194,16 +190,32 @@
     act[me] = activated
     dsil[...] = sigmoid * (1.0 + latent * (1.0 - sigmoid))
 
+    def forecast(e, first=False):
+        cols = pl.ds(pl.multiple_of(e * blk, blk), blk)
+        adapter = x_ref[:, cols].astype(F32) + matmul_nt(act[me], wu[e])
+        part = matmul(adapter.astype(BF16), ro[e])
+        est[...] = part if first else est[...] + part
+
     @pl.when(sec == last)
     def _():
         copy_to(ro.at[pl.ds(0, ndp - 1)], ro.at[pl.ds(0, ndp - 1)], ro_send, ro_recv, at(mx, my)).wait_recv()
-        hidden = act[me]
-        est = jnp.zeros((ntok, ro.shape[2]), F32)
-        for b in range(ndp):
-            cols = slice(b * blk, (b + 1) * blk)
-            adapter = x_ref[:, cols].astype(F32) + matmul_nt(hidden, wu[b])
-            est = est + matmul(adapter.astype(BF16), ro[b])
-        diff = est - gt_ref[...]
+        forecast(me, True)
+        for row in order[1:]:
+            forecast(column(0, row))
+        for row in order:
+            forecast(column(1, row))
+
+    for shift in (-1, 2):
+        for row in order:
+            wait_block(column(shift, row), 1)
+
+            @pl.when(sec == last)
+            def _(shift=shift, row=row):
+                forecast(column(shift, row))
+
+    @pl.when(sec == last)
+    def _():
+        diff = est[...] - gt_ref[...]
         offset = lax.broadcasted_iota(jnp.int32, (rows, diff.shape[1]), 0)
         errs = []
         for m in range(nmb):
@@ -319,6 +331,8 @@
 
     def stretch(g, c):
         lax.fori_loop(g * GROUP, (g + 1) * GROUP, step, 0)
+        part = pl.ds(g * GROUP, GROUP)
+        pltpu.make_async_copy(outp.at[part], out_ref.at[part], out_sem).start()
         pass_on(g)
         return c
 
@@ -332,7 +346,6 @@
 
     own = pltpu.make_async_copy(inc.at[:, :, own_cols], cot.at[me], own_sem)
     own.start()
-    out_ref[...] = outp[...].reshape(ntok, width)
     own.wait()
 
     others = pl.ds(0, ndp - 1)
@@ -352,6 +365,7 @@
     dg = matmul_tn(ncols[...].reshape(ndp * ntok, blk), lg[...].reshape(ndp * ntok, latw))
     dg_ref[...] = dg.astype(BF16)
 
+    pltpu.make_async_copy(outp, out_ref, out_sem).wait()
     for k in (0, 1):
         copy_to(pieces[k].at[others], pieces[k].at[others], w_send, w_recv.at[k, 0], at(mx, my)).wait_send()
 
@@ -372,6 +386,34 @@
             return c
 
         lax.fori_loop(0, nmb, gone, 0)
+
+
+def hand_over_kernel(pieces, a_in, b_in, c_in, a_out, b_out, c_out, a_buf, b_buf, c_buf, in_sem, out_sem):
+    rows = a_buf.shape[0] // pieces
+    jobs = [(b_in, b_buf, b_out), (c_in, c_buf, c_out)]
+    for i in range(pieces):
+        part = pl.ds(i * rows, rows)
+        jobs.append((a_in.at[part], a_buf.at[part], a_out.at[part]))
+    for i, (src, buf, _) in enumerate(jobs):
+        pltpu.make_async_copy(src, buf, in_sem.at[i]).start()
+    for i, (src, buf, dst) in enumerate(jobs):
+        pltpu.make_async_copy(src, buf, in_sem.at[i]).wait()
+        pltpu.make_async_copy(buf, dst, out_sem.at[i]).start()
+    for i, (_, buf, dst) in enumerate(jobs):
+        pltpu.make_async_copy(buf, dst, out_sem.at[i]).wait()
+
+
+def hand_over(*arrays, pieces=4):
+    anywhere = pl.BlockSpec(memory_space=pl.ANY)
+    return pl.pallas_call(
+        functools.partial(hand_over_kernel, pieces),
+        name="hand_over",
+        out_shape=tuple(jax.ShapeDtypeStruct(a.shape, a.dtype) for a in arrays),
+        in_specs=[anywhere] * 3,
+        out_specs=(anywhere,) * 3,
+        scratch_shapes=[pltpu.VMEM(a.shape, a.dtype) for a in arrays]
+        + [pltpu.SemaphoreType.DMA((2 + pieces,)), pltpu.SemaphoreType.DMA((2 + pieces,))],
+    )(*arrays)
 
 
 def per_device(
@@ -388,12 +430,12 @@
         functools.partial(kernel, ndp, nsec),
         name="relay",
         out_shape=(
-            jax.ShapeDtypeStruct((ntok, width), BF16),
+            jax.ShapeDtypeStruct((nmb, rows, width), BF16),
             jax.ShapeDtypeStruct((blk, latw), BF16),
             jax.ShapeDtypeStruct((latw, blk), BF16),
         ),
         in_specs=[vmem] * 6 + [pl.BlockSpec(memory_space=pltpu.SMEM)],
-        out_specs=(vmem, vmem, vmem),
+        out_specs=(pl.BlockSpec(memory_space=pl.ANY), vmem, vmem),
         scratch_shapes=[
             pltpu.VMEM((ndp, latw, blk), BF16),
             pltpu.VMEM((ndp, blk, latw), BF16),
@@ -408,6 +450,7 @@
             pltpu.VMEM((ndp, nmb, rows, latw), BF16),
             pltpu.VMEM((ndp, nmb, rows, blk), BF16),
             pltpu.VMEM((nmb, rows, width), BF16),
+            pltpu.VMEM((ntok, horizon), F32),
             dma,
             dma((2, ndp)),
             dma,
@@ -422,6 +465,7 @@
             dma((ndp, nmb // GROUP)),
             dma((nmb, SPLIT)),
             dma((nmb, SPLIT)),
+            dma,
             dma,
             pltpu.SemaphoreType.REGULAR,
         ],
@@ -435,6 +479,7 @@
         ground_truth_series,
         valid_len,
     )
+    grads, dg, ug = hand_over(grads.reshape(ntok, width), dg, ug)
     return grads[None], dg[None], ug[None]
 
 

time: 233 us -> 223 us (0.957)
  Pallas kernels: 228 us -> 222 us
  local copies, waits for them, and re-layouts: 3.93 us -> 0 us
    pallas_call x1, Pallas kernels: 228 us -> 220 us  [per_device(): pl.pallas_call(functools.partial(kernel, ndp, nsec), name='relay', out_sh...]
    unnamed x7 -> x0, local copies, waits for them, and re-layouts: 3.93 us -> none
where the time goes in v3:
time: 223 us
  Pallas kernels  222 us (100%)
    pallas_call x1, Pallas kernels, per_device(): pl.pallas_call(functools.partial(kernel, ndp, nsec), name='relay', out_sh...  220 us

profile of v3, /device:TPU:2, one launch (start us, length us, event | category | flops | bytes accessed | tf_op | source)
XLA Modules:
  0.0 223.0 jit_solution(6728026639975140224)
XLA Ops:
  0.6 220.2 %relay.1 = (bf16[8,16,4096]{2,1,0:T(8,128)(2,1)}, bf16[256,256]{1,0:T(8,128)(2,1)}, bf16[256,256]{1,0:T(8,128)(2,1)}) custom-call(bf16[128,4096]{1,0:T(8,128)(2,1)} %bitcast.8, bf16[1,4096]{1,0:T(2,128)(2,1)} %gain_ref.1, bf16[256,256]{1,0:T(8,128)(2,1)} %bitcast.9, bf16[256,256]{1,0:T(8,128)(2,1)} %bitcast.10, bf16[256,128]{1,0:T(8,128)(2,1)} %ro_ref.1, ...), custom_call_target="tpu_custom_call" | custom-call | tf_op jit(solution)/shard_map/relay/pallas_call | solution.py:429
  220.8 2.1 hand_over.1

commit v4 on v3

--- a/solution.py
+++ b/solution.py
@@ -13,9 +13,11 @@
 BF16 = jnp.bfloat16
 LINE = 4
 GROUP = 2
+SIDE = 128
+LAG = 2
 TOP = 8
 SPLIT = 4
-COT_GROUPS = 2
+COT_GROUPS = 1
 
 
 def matmul(left, right):
@@ -63,6 +65,7 @@
     cot,
     outp,
     est,
+    cot_next,
     w_send,
     w_recv,
     ro_send,
@@ -79,6 +82,8 @@
     r_recv,
     own_sem,
     out_sem,
+    x_send,
+    x_recv,
     clear,
 ):
     nmb, rows, width = inc.shape
@@ -141,6 +146,7 @@
         return ((mx + shift + ncol) % ncol) * LINE + row
 
     even = sec % 2 == 0
+    odd = sec % 2 == 1
 
 
     for k in (0, 1):
@@ -266,9 +272,11 @@
             for b in range(q * per, (q + 1) * per):
                 h = h + matmul(inc[m, :, b * blk : (b + 1) * blk], wu[b])
         latent_grad = (h * dsil[tok, :]).astype(BF16)
-        lg[me, m] = latent_grad
+        lg[me, m, :, 0:latw] = latent_grad
         iv = inv[tok, 0:1]
         mean = jnp.sum(latent_grad.astype(F32) * lat[tok, :], axis=-1, keepdims=True) * (1.0 / width)
+        lane = lax.broadcasted_iota(jnp.int32, (rows, SIDE), 1)
+        lg[me, m, :, latw:] = jnp.where(lane < SIDE // 2, iv, iv * mean).astype(BF16)
         for q in range(SPLIT):
             for b in range(q * per, (q + 1) * per):
                 cols = slice(b * blk, (b + 1) * blk)
@@ -300,8 +308,7 @@
             send_lg(me, g, right)
             for row in order[1:]:
                 send_lg(me, g, at(mx, row))
-        @pl.when((g < groups) & (g % COT_GROUPS == COT_GROUPS - 1))
-        def _():
+        def send_columns():
             part = pl.ds((g + 1 - COT_GROUPS) * GROUP, GROUP * COT_GROUPS)
 
             def send_cot(j, c):
@@ -312,20 +319,24 @@
 
             lax.fori_loop(1, ndp, send_cot, 0)
 
-        @pl.when((g >= 1) & (g <= groups))
+        @pl.when((g < groups) & (g % COT_GROUPS == COT_GROUPS - 1))
+        def _():
+            pl.when(odd)(send_columns)
+
+        @pl.when((g >= LAG) & (g < groups + LAG))
         def _():
             for row in order[1:]:
-                wait_lg(column(0, row), g - 1)
-                send_lg(column(0, row), g - 1, left)
-                send_lg(column(0, row), g - 1, right)
-
-        @pl.when(g >= 2)
+                wait_lg(column(0, row), g - LAG)
+                send_lg(column(0, row), g - LAG, left)
+                send_lg(column(0, row), g - LAG, right)
+
+        @pl.when(g >= 2 * LAG)
         def _():
             for n, row in enumerate(order):
                 near = 1 if n % 2 else -1
                 e = column(near, row)
-                wait_lg(e, g - 2)
-                send_lg(e, g - 2, left if n % 2 else right)
+                wait_lg(e, g - 2 * LAG)
+                send_lg(e, g - 2 * LAG, left if n % 2 else right)
 
     groups = nmb // GROUP
 
@@ -337,22 +348,21 @@
         return c
 
     lax.fori_loop(0, groups, stretch, 0)
-    pass_on(groups)
-    pass_on(groups + 1)
+    for g in range(groups, groups + 2 * LAG):
+        pass_on(g)
 
     @pl.when(sec >= nsec - TOP)
     def _():
         lax.fori_loop(1, ndp, send_early, 0)
 
     own = pltpu.make_async_copy(inc.at[:, :, own_cols], cot.at[me], own_sem)
-    own.start()
-    own.wait()
+
+    @pl.when(odd)
+    def _():
+        own.start()
+        own.wait()
 
     others = pl.ds(0, ndp - 1)
-    copy_to(act.at[others], act.at[others], a_send, a_recv, at(mx, my)).wait_recv()
-    copy_to(ncols.at[others], ncols.at[others], n_send, n_recv, at(mx, my)).wait_recv()
-    copy_to(cot.at[others], cot.at[others], c_send, c_recv, at(mx, my)).wait_recv()
-
     def last_lg(g, c):
         for n, row in enumerate(order):
             wait_lg(column(-1 if n % 2 else 1, row), g)
@@ -360,10 +370,38 @@
         return c
 
     lax.fori_loop(0, groups, last_lg, 0)
+    copy_to(ncols.at[others], ncols.at[others], n_send, n_recv, at(mx, my)).wait_recv()
+
+    def ship(e):
+        return copy_to(cot_next.at[e], cot.at[e], x_send, x_recv, below)
+
+    @pl.when(odd)
+    def _():
+        copy_to(cot.at[others], cot.at[others], c_send, c_recv, at(mx, my)).wait_recv()
+        gain_own = gain_ref[:, own_cols].astype(F32)
+        gain_inv = 1.0 / gain_own
+
+        def next_cols(e, c):
+            side = lg[e, :, :, latw:].reshape(ntok, SIDE).astype(F32)
+            scaled = matmul(lg[e, :, :, 0:latw].reshape(ntok, latw), wd[me]) * gain_own
+            unit = ncols[e].astype(F32) * gain_inv
+            grad = cot[e].reshape(ntok, blk).astype(F32) + side[:, 0:1] * scaled - side[:, SIDE // 2 : SIDE // 2 + 1] * unit
+            cot_next[e] = grad.astype(BF16).reshape(nmb, rows, blk)
+            ship(e).start()
+            return c
+
+        lax.fori_loop(0, ndp, next_cols, 0)
+
+    dg = matmul_tn(ncols[...].reshape(ndp * ntok, blk), lg[:, :, :, 0:latw].reshape(ndp * ntok, latw))
+    dg_ref[...] = dg.astype(BF16)
+    copy_to(act.at[others], act.at[others], a_send, a_recv, at(mx, my)).wait_recv()
+
+    @pl.when(even)
+    def _():
+        copy_to(cot, cot, x_send, x_recv, below).wait_recv()
+
     ug = matmul_tn(act[...].reshape(ndp * ntok, latw), cot[...].reshape(ndp * ntok, blk))
     ug_ref[...] = ug.astype(BF16)
-    dg = matmul_tn(ncols[...].reshape(ndp * ntok, blk), lg[...].reshape(ndp * ntok, latw))
-    dg_ref[...] = dg.astype(BF16)
 
     pltpu.make_async_copy(outp, out_ref, out_sem).wait()
     for k in (0, 1):
@@ -375,7 +413,12 @@
 
     copy_to(act.at[others], act.at[others], a_send, a_recv, at(mx, my)).wait_send()
     copy_to(ncols.at[others], ncols.at[others], n_send, n_recv, at(mx, my)).wait_send()
-    copy_to(cot.at[others], cot.at[others], c_send, c_recv, at(mx, my)).wait_send()
+
+    @pl.when(odd)
+    def _():
+        copy_to(cot.at[others], cot.at[others], c_send, c_recv, at(mx, my)).wait_send()
+        copy_to(cot_next, cot, x_send, x_recv, below).wait_send()
+
     copy_to(lg.at[others], lg.at[others], l_send, l_recv.at[0, 0], left).wait_send()
 
     @pl.when(sec > 0)
@@ -447,10 +490,11 @@
             pltpu.VMEM((ntok, latw), F32),
             pltpu.VMEM((ntok, 128), F32),
             pltpu.VMEM((nmb, rows, width), BF16),
-            pltpu.VMEM((ndp, nmb, rows, latw), BF16),
+            pltpu.VMEM((ndp, nmb, rows, latw + SIDE), BF16),
             pltpu.VMEM((ndp, nmb, rows, blk), BF16),
             pltpu.VMEM((nmb, rows, width), BF16),
             pltpu.VMEM((ntok, horizon), F32),
+            pltpu.VMEM((ndp, nmb, rows, blk), BF16),
             dma,
             dma((2, ndp)),
             dma,
@@ -465,6 +509,8 @@
             dma((ndp, nmb // GROUP)),
             dma((nmb, SPLIT)),
             dma((nmb, SPLIT)),
+            dma,
+            dma,
             dma,
             dma,
             pltpu.SemaphoreType.REGULAR,

time: 223 us -> 220 us (0.987)
  the two profiles are of different devices: /device:TPU:2 before, /device:TPU:8 now
where the time goes in v4:
time: 220 us
  Pallas kernels  219 us (100%)
    pallas_call x1, Pallas kernels, per_device(): pl.pallas_call(functools.partial(kernel, ndp, nsec), name='relay', out_sh...  217 us

profile of v4, /device:TPU:8, one launch (start us, length us, event | category | flops | bytes accessed | tf_op | source)
XLA Modules:
  0.0 220.0 jit_solution(4864626821432771328)
XLA Ops:
  0.6 217.2 %relay.1 = (bf16[8,16,4096]{2,1,0:T(8,128)(2,1)}, bf16[256,256]{1,0:T(8,128)(2,1)}, bf16[256,256]{1,0:T(8,128)(2,1)}) custom-call(bf16[128,4096]{1,0:T(8,128)(2,1)} %bitcast.8, bf16[1,4096]{1,0:T(2,128)(2,1)} %gain_ref.1, bf16[256,256]{1,0:T(8,128)(2,1)} %bitcast.9, bf16[256,256]{1,0:T(8,128)(2,1)} %bitcast.10, bf16[256,128]{1,0:T(8,128)(2,1)} %ro_ref.1, ...), custom_call_target="tpu_custom_call" | custom-call | tf_op jit(solution)/shard_map/relay/pallas_call | solution.py:472
  217.9 2.1 hand_over.1

commit v5 on v4

--- a/solution.py
+++ b/solution.py
@@ -12,11 +12,12 @@
 F32 = jnp.float32
 BF16 = jnp.bfloat16
 LINE = 4
-GROUP = 2
+ROWS = 8
+GROUP = 4
 SIDE = 128
 LAG = 2
 TOP = 8
-SPLIT = 4
+SPLIT = 2
 COT_GROUPS = 1
 
 
@@ -30,6 +31,10 @@
 
 def matmul_tn(left, right):
     return lax.dot_general(left, right, (((0,), (0,)), ((), ())), preferred_element_type=F32)
+
+
+def flat(values, rows):
+    return values.astype(F32).reshape(rows, values.shape[-1]).astype(BF16)
 
 
 def copy_to(src, dst, send, recv, dev):
@@ -164,12 +169,12 @@
         lax.fori_loop(1, ndp, send_ro, 0)
 
     gain = gain_ref[...].astype(F32)
-    values = x_ref[...].astype(F32)
+    values = x_ref[...].astype(F32).reshape(ntok, width)
     inverse = lax.rsqrt(jnp.mean(values * values, axis=-1, keepdims=True) + EPSILON)
     inv[...] = jnp.broadcast_to(inverse, inv.shape)
     for b in range(ndp):
         cols = slice(b * blk, (b + 1) * blk)
-        unit = x_ref[:, cols].astype(F32) * inverse
+        unit = x_ref[:, :, cols].astype(F32).reshape(ntok, blk) * inverse
         normed[b] = (unit * gain[:, cols]).astype(BF16)
 
     for k, near, way in ((0, -1, right), (1, 1, left)):
@@ -198,7 +203,7 @@
 
     def forecast(e, first=False):
         cols = pl.ds(pl.multiple_of(e * blk, blk), blk)
-        adapter = x_ref[:, cols].astype(F32) + matmul_nt(act[me], wu[e])
+        adapter = x_ref[:, :, cols].astype(F32).reshape(ntok, blk) + matmul_nt(act[me], wu[e])
         part = matmul(adapter.astype(BF16), ro[e])
         est[...] = part if first else est[...] + part
 
@@ -222,16 +227,17 @@
     @pl.when(sec == last)
     def _():
         diff = est[...] - gt_ref[...]
-        offset = lax.broadcasted_iota(jnp.int32, (rows, diff.shape[1]), 0)
+        micro = ntok // vl_ref.shape[0]
+        offset = lax.broadcasted_iota(jnp.int32, (micro, diff.shape[1]), 0)
         errs = []
-        for m in range(nmb):
+        for m in range(vl_ref.shape[0]):
             mask = jnp.where(offset < vl_ref[m], 1.0, 0.0)
-            errs.append(mask * diff[m * rows : (m + 1) * rows])
+            errs.append(mask * diff[m * micro : (m + 1) * micro])
         error = jnp.concatenate(errs, axis=0).astype(BF16)
         for b in range(ndp):
             cols = slice(b * blk, (b + 1) * blk)
-            top = matmul_nt(error, ro[b]).astype(BF16)
-            inc[:, :, cols] = top.reshape(nmb, rows, blk)
+            top = matmul_nt(error, ro[b])
+            inc[:, :, cols] = top.reshape(nmb, rows, blk).astype(BF16)
 
     def send_early(j, c):
         p = peer(j)
@@ -281,7 +287,7 @@
             for b in range(q * per, (q + 1) * per):
                 cols = slice(b * blk, (b + 1) * blk)
                 scaled = matmul(latent_grad, wd[b]) * gain_ref[:, cols].astype(F32)
-                unit = x_ref[tok, cols].astype(F32) * iv
+                unit = x_ref[m, :, cols].astype(F32) * iv
                 g = inc[m, :, cols].astype(F32) + iv * (scaled - unit * mean)
                 outp[m, :, cols] = g.astype(BF16)
 
@@ -382,17 +388,17 @@
         gain_inv = 1.0 / gain_own
 
         def next_cols(e, c):
-            side = lg[e, :, :, latw:].reshape(ntok, SIDE).astype(F32)
-            scaled = matmul(lg[e, :, :, 0:latw].reshape(ntok, latw), wd[me]) * gain_own
+            side = lg[e, :, :, latw:].astype(F32).reshape(ntok, SIDE)
+            scaled = matmul(flat(lg[e, :, :, 0:latw], ntok), wd[me]) * gain_own
             unit = ncols[e].astype(F32) * gain_inv
-            grad = cot[e].reshape(ntok, blk).astype(F32) + side[:, 0:1] * scaled - side[:, SIDE // 2 : SIDE // 2 + 1] * unit
-            cot_next[e] = grad.astype(BF16).reshape(nmb, rows, blk)
+            grad = cot[e].astype(F32).reshape(ntok, blk) + side[:, 0:1] * scaled - side[:, SIDE // 2 : SIDE // 2 + 1] * unit
+            cot_next[e] = grad.reshape(nmb, rows, blk).astype(BF16)
             ship(e).start()
             return c
 
         lax.fori_loop(0, ndp, next_cols, 0)
 
-    dg = matmul_tn(ncols[...].reshape(ndp * ntok, blk), lg[:, :, :, 0:latw].reshape(ndp * ntok, latw))
+    dg = matmul_tn(ncols[...].reshape(ndp * ntok, blk), flat(lg[:, :, :, 0:latw], ndp * ntok))
     dg_ref[...] = dg.astype(BF16)
     copy_to(act.at[others], act.at[others], a_send, a_recv, at(mx, my)).wait_recv()
 
@@ -400,7 +406,7 @@
     def _():
         copy_to(cot, cot, x_send, x_recv, below).wait_recv()
 
-    ug = matmul_tn(act[...].reshape(ndp * ntok, latw), cot[...].reshape(ndp * ntok, blk))
+    ug = matmul_tn(act[...].reshape(ndp * ntok, latw), flat(cot[...], ndp * ntok))
     ug_ref[...] = ug.astype(BF16)
 
     pltpu.make_async_copy(outp, out_ref, out_sem).wait()
@@ -465,8 +471,8 @@
     _, ntok, width = section_inputs.shape
     _, blk, latw = down_proj.shape
     horizon = readout_matrix.shape[1]
-    nmb = valid_len.shape[0]
-    rows = ntok // nmb
+    rows = ROWS
+    nmb = ntok // rows
     vmem = pl.BlockSpec(memory_space=pltpu.VMEM)
     dma = pltpu.SemaphoreType.DMA
     grads, dg, ug = pl.pallas_call(
@@ -517,7 +523,7 @@
         ],
         compiler_params=pltpu.CompilerParams(collective_id=0, has_side_effects=True),
     )(
-        section_inputs[0],
+        section_inputs.reshape(nmb, rows, width),
         norm_gain,
         down_proj[0],
         up_proj[0],

time: 220 us -> 217 us (0.986)
  Pallas kernels: 219 us -> 216 us
    pallas_call x1, Pallas kernels: 217 us -> 214 us  [per_device(): pl.pallas_call(functools.partial(kernel, ndp, nsec), name='relay', out_sh...]
where the time goes in v5:
time: 217 us
  Pallas kernels  216 us (100%)
    pallas_call x1, Pallas kernels, per_device(): pl.pallas_call(functools.partial(kernel, ndp, nsec), name='relay', out_sh...  214 us

profile of v5, /device:TPU:8, one launch (start us, length us, event | category | flops | bytes accessed | tf_op | source)
XLA Modules:
  0.0 216.7 jit_solution(5560225043116968364)
XLA Ops:
  0.6 213.9 %relay.1 = (bf16[16,8,4096]{2,1,0:T(8,128)(2,1)}, bf16[256,256]{1,0:T(8,128)(2,1)}, bf16[256,256]{1,0:T(8,128)(2,1)}) custom-call(bf16[16,8,4096]{2,1,0:T(8,128)(2,1)} %bitcast.8, bf16[1,4096]{1,0:T(2,128)(2,1)} %gain_ref.1, bf16[256,256]{1,0:T(8,128)(2,1)} %bitcast.9, bf16[256,256]{1,0:T(8,128)(2,1)} %bitcast.10, bf16[256,128]{1,0:T(8,128)(2,1)} %ro_ref.1, ...), custom_call_target="tpu_custom_call" | custom-call | tf_op jit(solution)/shard_map/relay/pallas_call | solution.py:478
  214.6 2.1 hand_over.1

commit v6 on v5

--- a/solution.py
+++ b/solution.py
@@ -13,9 +13,9 @@
 BF16 = jnp.bfloat16
 LINE = 4
 ROWS = 8
-GROUP = 4
+GROUP = 2
 SIDE = 128
-LAG = 2
+LAG = 3
 TOP = 8
 SPLIT = 2
 COT_GROUPS = 1

time: 217 us -> 218 us (level)
  the two profiles are of different devices: /device:TPU:8 before, /device:TPU:2 now
where the time goes in v6:
time: 218 us
  Pallas kernels  217 us (100%)
    pallas_call x1, Pallas kernels, per_device(): pl.pallas_call(functools.partial(kernel, ndp, nsec), name='relay', out_sh...  215 us

profile of v6, /device:TPU:2, one launch (start us, length us, event | category | flops | bytes accessed | tf_op | source)
XLA Modules:
  0.0 217.6 jit_solution(2831828137183165383)
XLA Ops:
  0.6 214.8 %relay.1 = (bf16[16,8,4096]{2,1,0:T(8,128)(2,1)}, bf16[256,256]{1,0:T(8,128)(2,1)}, bf16[256,256]{1,0:T(8,128)(2,1)}) custom-call(bf16[16,8,4096]{2,1,0:T(8,128)(2,1)} %bitcast.8, bf16[1,4096]{1,0:T(2,128)(2,1)} %gain_ref.1, bf16[256,256]{1,0:T(8,128)(2,1)} %bitcast.9, bf16[256,256]{1,0:T(8,128)(2,1)} %bitcast.10, bf16[256,128]{1,0:T(8,128)(2,1)} %ro_ref.1, ...), custom_call_target="tpu_custom_call" | custom-call | tf_op jit(solution)/shard_map/relay/pallas_call | solution.py:478
  215.5 2.1 hand_over.1
